TPU v7x, 512 devices: a whole 4x4x16 slice. The times are simulated.
512 devices in a mesh: dp: 32 (over y, x, core), ctx: 16 (over z).
Axes of the slice: x: 4, y: 4, z: 16, core: 2. Of those that a mesh axis runs over, the one named last changes fastest.
Arguments:
- layer_input: bfloat16 [32, 2048, 1024], P('dp', 'ctx'), may hold values from -6 to 6
- projected: bfloat16 [32, 2048, 3072], P('dp', 'ctx'), may hold values from -6 to 6
- grad_output: bfloat16 [32, 2048, 1024], P('dp', 'ctx'), may hold values from -12 to 12
- w_qkv: bfloat16 [1024, 3072], P('dp', 'ctx'), may hold values from -0.1875 to 0.1875
- lengths: int32 [32, 8], P('dp'), may hold values from 1 to 1024, 2048 in all within a row
- block_perm: int32 [32, 16], P('dp'), may hold values from 0 to 15, each once within a row
Outputs:
- grad_input: bfloat16 [32, 2048, 1024], P('dp', 'ctx')
- grad_weight: float32 [1024, 3072], P('dp', 'ctx')
Inputs may be any that keep to these rules, and one draw needn't show every extreme that they name: Every row of lengths sums to 2048 and has an entry equal to 1024. Every row of block_perm names each of the 16 blocks once; slot block s holds packed positions block_perm[g, s] * 128 to block_perm[g, s] * 128 + 127.
All inputs are finite; a program needn't handle non-finite values.
Results may differ from a plain program's by a relative error of at most 0.0065.
Values may be sent and summed in bfloat16 or wider, within the bound.
A program may use at most 64 MiB of HBM per device.

v0:
```python
import jax
import jax.numpy as jnp
from jax import lax
from jax.sharding import PartitionSpec as P

DH = 64


def silu_slope(value):
    sigma = jax.nn.sigmoid(value)
    return sigma * (1.0 + value * (1.0 - sigma))


def slot_positions(slot_blocks, rows, block_size):
    slots = jnp.arange(rows, dtype=jnp.int32)
    owner = (slots // block_size)[:, None] == jnp.arange(slot_blocks.shape[0], dtype=jnp.int32)[
        None, :
    ]
    placed = jnp.sum(jnp.where(owner, slot_blocks[None, :], 0), axis=1)
    return placed * block_size + slots % block_size


def user_layout(user_lengths, position):
    ends = jnp.cumsum(user_lengths)
    segment = jnp.sum((position[:, None] >= ends[None, :]).astype(jnp.int32), axis=1)
    member = segment[:, None] == jnp.arange(user_lengths.shape[0], dtype=jnp.int32)[None, :]
    user_len = jnp.sum(jnp.where(member, user_lengths[None, :], 0), axis=1)
    first_row = jnp.sum(jnp.where(member, (ends - user_lengths)[None, :], 0), axis=1)
    row_scale = lax.rsqrt(user_len.astype(jnp.float32))
    return (segment, row_scale, first_row)


def rounded_term(term):
    return lax.optimization_barrier(term.astype(jnp.bfloat16)).astype(jnp.float32)


def tile_grads(
    query_block,
    grad_block,
    position_block,
    segment_block,
    scale_block,
    key_block,
    value_block,
    key_position,
    key_segment,
):
    scale = DH ** (-0.5)
    contract = (((1,), (1,)), ((), ()))
    across = (((0,), (0,)), ((), ()))
    scores = (
        lax.dot_general(query_block, key_block, contract, preferred_element_type=jnp.float32)
        * scale
    )
    visible = (segment_block[:, None] == key_segment[None, :]) & (
        key_position[None, :] <= position_block[:, None]
    )
    sigma = jax.nn.sigmoid(scores)
    weights = jnp.where(visible, scores * sigma * scale_block[:, None], 0.0).astype(jnp.bfloat16)
    grad_weights = lax.dot_general(
        grad_block, value_block, contract, preferred_element_type=jnp.float32
    )
    slope = grad_weights * sigma * (1.0 + scores * (1.0 - sigma)) * (scale_block[:, None] * scale)
    grad_scores = jnp.where(visible, slope, 0.0).astype(jnp.bfloat16)
    grad_query = jnp.dot(grad_scores, key_block, preferred_element_type=jnp.float32)
    grad_key = lax.dot_general(grad_scores, query_block, across, preferred_element_type=jnp.float32)
    grad_value = lax.dot_general(weights, grad_block, across, preferred_element_type=jnp.float32)
    return (grad_query, grad_key, grad_value)


def dense_grads(
    query_rows, key_rows, value_rows, grad_rows, position, segment, row_scale, block_rows
):
    whole = query_rows.shape[0]
    count = whole // block_rows

    def blocked(array):
        return array.reshape((count, block_rows) + array.shape[1:])

    def step(carry, block_item):
        query_block, grad_block, position_block, segment_block, scale_block = block_item
        grad_query, grad_key, grad_value = tile_grads(
            query_block,
            grad_block,
            position_block,
            segment_block,
            scale_block,
            key_rows,
            value_rows,
            position,
            segment,
        )
        return ((carry[0] + grad_key, carry[1] + grad_value), grad_query)

    empty = jnp.zeros((whole, DH), jnp.float32)
    sums, grad_query = lax.scan(
        step,
        (empty, empty),
        (
            blocked(query_rows),
            blocked(grad_rows),
            blocked(position),
            blocked(segment),
            blocked(row_scale),
        ),
    )
    return (grad_query.reshape(whole, DH), sums[0], sums[1])


def body(layer_input, projected, grad_output, w_qkv, lengths, block_perm):
    tokens_dev = layer_input.shape[1]
    width = layer_input.shape[2]
    ctx_count = lax.axis_size("ctx")
    data_count = lax.axis_size("dp")
    whole = tokens_dev * ctx_count
    local_heads = width // DH // ctx_count
    columns = local_heads * 3 * DH
    user_lengths = lengths[0]
    slot_blocks = block_perm[0]
    block_size = whole // slot_blocks.shape[0]
    block_rows = min(512, whole)
    position = slot_positions(slot_blocks, whole, block_size)
    segment, row_scale, first_row = user_layout(user_lengths, position)
    contract_cols = (((1,), (1,)), ((), ()))

    def one_head(pre_head, grad_head):
        active = jax.nn.silu(pre_head.astype(jnp.float32)).astype(jnp.bfloat16)
        query_rows = active[:, :DH]
        key_rows = active[:, DH : 2 * DH]
        value_rows = active[:, 2 * DH :]
        grad_query, grad_key, grad_value = dense_grads(
            query_rows, key_rows, value_rows, grad_head, position, segment, row_scale, block_rows
        )
        grads = jnp.concatenate([grad_query, grad_key, grad_value], axis=1)
        return (grads * silu_slope(pre_head.astype(jnp.float32))).astype(jnp.bfloat16)

    pre_split = projected[0].reshape(tokens_dev, ctx_count, local_heads, 3 * DH)
    grad_split = grad_output[0].reshape(tokens_dev, ctx_count, local_heads, DH)
    pre_pieces = lax.all_to_all(pre_split, "ctx", split_axis=1, concat_axis=0, tiled=True)
    grad_pieces = lax.all_to_all(grad_split, "ctx", split_axis=1, concat_axis=0, tiled=True)
    grad_pre = jax.vmap(one_head, in_axes=(1, 1), out_axes=1)(pre_pieces[:, 0], grad_pieces[:, 0])
    flat_grad = grad_pre.reshape(whole, columns)
    weight_local = lax.dot_general(
        lax.all_gather(layer_input, "ctx", axis=1, tiled=True)[0],
        flat_grad,
        (((0,), (0,)), ((), ())),
        preferred_element_type=jnp.float32,
    )
    grad_weight = lax.psum_scatter(weight_local, "dp", scatter_dimension=0, tiled=True) * (
        1.0 / data_count
    )
    token_grad = lax.all_to_all(flat_grad, "ctx", split_axis=0, concat_axis=1, tiled=True)
    weight_cols_band = lax.all_gather(w_qkv, "dp", axis=0, tiled=True)
    input_sum = jnp.zeros((tokens_dev, width), jnp.float32)
    piece = lax.all_gather(weight_cols_band, "ctx", axis=1, tiled=True)
    for group in range(piece.shape[1] // columns):
        part = lax.dynamic_slice_in_dim(token_grad, group * columns, columns, 1)
        term = lax.dot_general(
            part,
            piece[:, group * columns : (group + 1) * columns],
            contract_cols,
            preferred_element_type=jnp.float32,
        )
        input_sum = input_sum + rounded_term(term)
    return (input_sum.astype(jnp.bfloat16)[None], grad_weight)


def solution(mesh):
    return jax.shard_map(
        body,
        mesh=mesh,
        in_specs=(
            P("dp", "ctx", None),
            P("dp", "ctx", None),
            P("dp", "ctx", None),
            P("dp", "ctx"),
            P("dp", None),
            P("dp", None),
        ),
        out_specs=(P("dp", "ctx", None), P("dp", "ctx")),
        check_vma=False,
    )
```

profile of v0, /device:TPU:1, one launch (start us, length us, event | category | flops | bytes accessed | tf_op | source)
XLA Modules:
  0.0 383.3 jit_solution(13756255645604176255)
XLA Ops:
  7.2 1.8 copy.87
  9.0 15.7 %all-to-all-start = ((bf16[128,16,1,64]{0,3,2,1:T(8,128)(2,1)}), bf16[128,16,1,64]{0,3,2,1:T(8,128)(2,1)S(1)}, u32[]{:S(2)}, u32[]{:S(2)}) async-start(bf16[128,16,1,64]{0,3,2,1:T(8,128)(2,1)} %bitcast.4), calls=%async_computation | async-start | bytes 524288 | tf_op jit(solution)/shard_map/all_to_all | solution.py:140
  24.7 2.3 copy.90
  27.0 11.5 %all-to-all-done = bf16[128,16,1,64]{0,3,2,1:T(8,128)(2,1)S(1)} async-done(((bf16[128,16,1,64]{0,3,2,1:T(8,128)(2,1)}), bf16[128,16,1,64]{0,3,2,1:T(8,128)(2,1)S(1)}, u32[]{:S(2)}, u32[]{:S(2)}) %all-to-all-start) | async-done | bytes 262176 | tf_op jit(solution)/shard_map/all_to_all | solution.py:140
  38.5 10.3 %all-to-all-start.1 = ((bf16[128,16,1,192]{0,3,2,1:T(8,128)(2,1)}), bf16[128,16,1,192]{0,3,2,1:T(8,128)(2,1)S(1)}, u32[]{:S(2)}, u32[]{:S(2)}) async-start(bf16[128,16,1,192]{0,3,2,1:T(8,128)(2,1)} %bitcast.9), calls=%async_computation.1 | async-start | bytes 1572864 | tf_op jit(solution)/shard_map/all_to_all | solution.py:139
  51.2 33.6 %all-to-all-done.1 = bf16[128,16,1,192]{0,3,2,1:T(8,128)(2,1)S(1)} async-done(((bf16[128,16,1,192]{0,3,2,1:T(8,128)(2,1)}), bf16[128,16,1,192]{0,3,2,1:T(8,128)(2,1)S(1)}, u32[]{:S(2)}, u32[]{:S(2)}) %all-to-all-start.1) | async-done | bytes 786464 | tf_op jit(solution)/shard_map/all_to_all | solution.py:139
  85.3 3.3 fusion.35
  88.6 1.6 fusion.84
  92.5 63.4 %while.15 = (s32[]{:T(128)}, f32[1,2048,64]{1,2,0:T(8,128)S(1)}, f32[1,2048,64]{1,2,0:T(8,128)}, f32[4,1,512,64]{2,0,3,1:T(4,128)}, s32[4,512]{1,0:T(4,128)S(1)}...) while((s32[]{:T(128)}, f32[1,2048,64]{1,2,0:T(8,128)S(1)}, ...), condition=%wide.region_5.6_spmd.clone, body=%wide.region_4.5_spmd.clone.sunk | while | flops 698876416 | bytes 43185944 | solution.py:96
  93.7 3.6 select_convert_fusion.6
  98.2 3.6 dynamic_update_slice.6
  101.8 1.5 fusion.109
  103.3 4.9 %fusion.110 = f32[1,2048,64]{1,2,0:T(8,128)} fusion(f32[512,2048]{1,0:T(8,128)} %copy-done, f32[512]{0:T(512)S(1)} %bitcast.200, s32[2048]{0:T(1024)S(1)} %get-tuple-element.347, s32[2048]{0:T(1024)S(1)} %get-tuple-element.346, s32[512]{0:T(512)S(1)} %bitcast.202, s32[512]{0:T(512)S(1)} %bitcast.204, f32[1,2048,64]{1,2,0:T(8,128)} %get-tuple-element.328, ...), kind=kOutput, calls=%fused_computation.5.clone.1 | convolution fusion | flops 146014208 | bytes 5396993 | tf_op jit(solution)/shard_map/vmap()/while/body/eval_jaxpr/dot_general | solution.py:67
  109.4 3.6 select_convert_fusion.6
  113.9 3.6 dynamic_update_slice.6
  117.6 1.5 fusion.109
  119.0 5.1 %fusion.110 = f32[1,2048,64]{1,2,0:T(8,128)} fusion(f32[512,2048]{1,0:T(8,128)} %copy-done, f32[512]{0:T(512)S(1)} %bitcast.200, s32[2048]{0:T(1024)S(1)} %get-tuple-element.347, s32[2048]{0:T(1024)S(1)} %get-tuple-element.346, s32[512]{0:T(512)S(1)} %bitcast.202, s32[512]{0:T(512)S(1)} %bitcast.204, f32[1,2048,64]{1,2,0:T(8,128)} %get-tuple-element.328, ...), kind=kOutput, calls=%fused_computation.5.clone.1 | convolution fusion | flops 146014208 | bytes 5396993 | tf_op jit(solution)/shard_map/vmap()/while/body/eval_jaxpr/dot_general | solution.py:67
  125.3 3.5 select_convert_fusion.6
  129.8 3.6 dynamic_update_slice.6
  133.5 1.5 fusion.109
  134.9 5.0 %fusion.110 = f32[1,2048,64]{1,2,0:T(8,128)} fusion(f32[512,2048]{1,0:T(8,128)} %copy-done, f32[512]{0:T(512)S(1)} %bitcast.200, s32[2048]{0:T(1024)S(1)} %get-tuple-element.347, s32[2048]{0:T(1024)S(1)} %get-tuple-element.346, s32[512]{0:T(512)S(1)} %bitcast.202, s32[512]{0:T(512)S(1)} %bitcast.204, f32[1,2048,64]{1,2,0:T(8,128)} %get-tuple-element.328, ...), kind=kOutput, calls=%fused_computation.5.clone.1 | convolution fusion | flops 146014208 | bytes 5396993 | tf_op jit(solution)/shard_map/vmap()/while/body/eval_jaxpr/dot_general | solution.py:67
  141.2 3.6 select_convert_fusion.6
  145.7 3.6 dynamic_update_slice.6
  149.3 1.5 fusion.109
  150.8 5.0 %fusion.110 = f32[1,2048,64]{1,2,0:T(8,128)} fusion(f32[512,2048]{1,0:T(8,128)} %copy-done, f32[512]{0:T(512)S(1)} %bitcast.200, s32[2048]{0:T(1024)S(1)} %get-tuple-element.347, s32[2048]{0:T(1024)S(1)} %get-tuple-element.346, s32[512]{0:T(512)S(1)} %bitcast.202, s32[512]{0:T(512)S(1)} %bitcast.204, f32[1,2048,64]{1,2,0:T(8,128)} %get-tuple-element.328, ...), kind=kOutput, calls=%fused_computation.5.clone.1 | convolution fusion | flops 146014208 | bytes 5396993 | tf_op jit(solution)/shard_map/vmap()/while/body/eval_jaxpr/dot_general | solution.py:67
  157.1 1.3 concatenate.26
  158.3 1.9 fusion.24
  160.3 3.2 fusion.36
  163.6 1.3 copy.107
  165.0 34.3 %all_gather.9 = bf16[1024,192]{1,0:T(8,128)(2,1)S(1)} all-gather(bf16[32,192]{1,0:T(8,128)(2,1)S(1)} %copy-done.7), channel_id=1, replica_groups=mesh['dp'=32,'ctx'=16] {'dp'}, dimensions={0}, use_global_device_ids=true | all-gather | bytes 405504 | tf_op jit(solution)/shard_map/all_gather | solution.py:153
  202.4 6.3 %all-to-all-start.2 = ((bf16[16,128,192]{1,2,0:T(8,128)(2,1)}), bf16[16,128,192]{1,2,0:T(8,128)(2,1)S(1)}, u32[]{:S(2)}, u32[]{:S(2)}) async-start(bf16[16,128,192]{1,2,0:T(8,128)(2,1)} %copy.98), calls=%async_computation.2 | async-start | bytes 1572864 | tf_op jit(solution)/shard_map/all_to_all | solution.py:152
  208.8 60.0 %reduce-scatter.4.cloned.1.call-done = f32[32,192]{1,0:T(8,128)} async-done(((f32[1024,192]{1,0:T(8,128)}), f32[32,192]{1,0:T(8,128)}) %reduce-scatter.4.cloned.1.call-update) | async-done | bytes 24592
  270.3 84.9 %all-gather.3.cloned.1.call-done = bf16[1024,3072]{0,1:T(8,128)(2,1)} async-done(((bf16[1024,192]{0,1:T(8,128)(2,1)}), bf16[1024,3072]{0,1:T(8,128)(2,1)}) %all-gather.3.cloned.1.call-update) | async-done | bytes 6291472 | tf_op jit(solution)/shard_map/all_gather | solution.py:155
  356.5 1.2 convolution_convert_fusion.14
  357.7 1.2 convolution_convert_fusion.13
  359.0 1.2 convolution_convert_fusion.12
  360.2 1.2 convolution_convert_fusion.11
  361.5 1.2 convolution_convert_fusion.10
  362.7 1.2 convolution_convert_fusion.9
  364.0 1.2 convolution_convert_fusion.8
  365.2 1.2 convolution_convert_fusion.7
  366.5 1.2 convolution_convert_fusion.6
  367.7 1.2 convolution_convert_fusion.5
  368.9 1.2 convolution_convert_fusion.4
  370.2 1.2 convolution_convert_fusion.3
  371.4 1.2 convolution_convert_fusion.2
  372.7 1.2 convolution_convert_fusion.1
  375.2 1.6 fusion.57
  (106 shorter events, 21.8 us)
Async XLA Ops:
  7.2 42.5 %copy-start.9 = (s32[1,8]{1,0:T(1,128)S(1)}, s32[1,8]{1,0:T(1,128)}, u32[]{:S(2)}) copy-start(s32[1,8]{1,0:T(1,128)} %param.12) | copy-start | bytes 100
  7.2 42.7 %copy-start.8 = (s32[1,16]{1,0:T(1,128)S(1)}, s32[1,16]{1,0:T(1,128)}, u32[]{:S(2)}) copy-start(s32[1,16]{1,0:T(1,128)} %param.13) | copy-start | bytes 196
  9.0 29.5 %all-to-all-start = ((bf16[128,16,1,64]{0,3,2,1:T(8,128)(2,1)}), bf16[128,16,1,64]{0,3,2,1:T(8,128)(2,1)S(1)}, u32[]{:S(2)}, u32[]{:S(2)}) async-start(bf16[128,16,1,64]{0,3,2,1:T(8,128)(2,1)} %bitcast.4), calls=%async_computation | async-start | bytes 524288 | tf_op jit(solution)/shard_map/all_to_all | solution.py:140
  38.5 46.3 %all-to-all-start.1 = ((bf16[128,16,1,192]{0,3,2,1:T(8,128)(2,1)}), bf16[128,16,1,192]{0,3,2,1:T(8,128)(2,1)S(1)}, u32[]{:S(2)}, u32[]{:S(2)}) async-start(bf16[128,16,1,192]{0,3,2,1:T(8,128)(2,1)} %bitcast.9), calls=%async_computation.1 | async-start | bytes 1572864 | tf_op jit(solution)/shard_map/all_to_all | solution.py:139
  48.8 111.5 %all-gather.5.cloned.1.call-start = ((), (), s32[]{:S(2)}) async-start(), calls=%async_computation.5 | async-start | bytes 4456448 | tf_op jit(solution)/shard_map/all_gather | solution.py:144
  49.6 219.2 %reduce-scatter.4.cloned.1.call-start = ((), (), s32[]{:S(2)}) async-start(), calls=%async_computation.6 | async-start | bytes 1081344
  84.8 5.4 %copy-start.1 = (bf16[128,16,1,192]{0,3,2,1:T(8,128)(2,1)}, bf16[128,16,1,192]{0,3,2,1:T(8,128)(2,1)S(1)}, u32[]{:S(2)}) copy-start(bf16[128,16,1,192]{0,3,2,1:T(8,128)(2,1)S(1)} %all-to-all-done.1) | copy-start | bytes 2359300
  92.5 0.8 copy-start.3
  92.5 1.2 copy-start.6
  93.2 4.1 %copy-start = (f32[512,2048]{1,0:T(8,128)}, f32[512,2048]{1,0:T(8,128)S(1)}, u32[]{:S(2)}) copy-start(f32[512,2048]{1,0:T(8,128)S(1)} %fusion.108) | copy-start | bytes 12582916 | tf_op jit(solution)/shard_map/vmap()/while
  103.3 4.9 %copy-start.4 = (bf16[4,1,512,64]{3,2,1,0:T(8,128)(2,1)S(1)}, bf16[4,1,512,64]{3,2,1,0:T(8,128)(2,1)}, u32[]{:S(2)}) copy-start(bf16[4,1,512,64]{3,2,1,0:T(8,128)(2,1)} %copy-done.3) | copy-start | bytes 786436 | tf_op jit(solution)/shard_map/vmap()/while
  108.2 0.8 copy-start.3
  108.2 1.2 copy-start.6
  108.9 4.1 %copy-start = (f32[512,2048]{1,0:T(8,128)}, f32[512,2048]{1,0:T(8,128)S(1)}, u32[]{:S(2)}) copy-start(f32[512,2048]{1,0:T(8,128)S(1)} %fusion.108) | copy-start | bytes 12582916 | tf_op jit(solution)/shard_map/vmap()/while
  119.0 5.1 %copy-start.4 = (bf16[4,1,512,64]{3,2,1,0:T(8,128)(2,1)S(1)}, bf16[4,1,512,64]{3,2,1,0:T(8,128)(2,1)}, u32[]{:S(2)}) copy-start(bf16[4,1,512,64]{3,2,1,0:T(8,128)(2,1)} %copy-done.3) | copy-start | bytes 786436 | tf_op jit(solution)/shard_map/vmap()/while
  124.1 0.8 copy-start.3
  124.1 1.2 copy-start.6
  124.8 4.1 %copy-start = (f32[512,2048]{1,0:T(8,128)}, f32[512,2048]{1,0:T(8,128)S(1)}, u32[]{:S(2)}) copy-start(f32[512,2048]{1,0:T(8,128)S(1)} %fusion.108) | copy-start | bytes 12582916 | tf_op jit(solution)/shard_map/vmap()/while
  134.9 5.1 %copy-start.4 = (bf16[4,1,512,64]{3,2,1,0:T(8,128)(2,1)S(1)}, bf16[4,1,512,64]{3,2,1,0:T(8,128)(2,1)}, u32[]{:S(2)}) copy-start(bf16[4,1,512,64]{3,2,1,0:T(8,128)(2,1)} %copy-done.3) | copy-start | bytes 786436 | tf_op jit(solution)/shard_map/vmap()/while
  140.0 0.8 copy-start.3
  140.0 1.2 copy-start.6
  140.7 4.1 %copy-start = (f32[512,2048]{1,0:T(8,128)}, f32[512,2048]{1,0:T(8,128)S(1)}, u32[]{:S(2)}) copy-start(f32[512,2048]{1,0:T(8,128)S(1)} %fusion.108) | copy-start | bytes 12582916 | tf_op jit(solution)/shard_map/vmap()/while
  150.8 5.1 %copy-start.4 = (bf16[4,1,512,64]{3,2,1,0:T(8,128)(2,1)S(1)}, bf16[4,1,512,64]{3,2,1,0:T(8,128)(2,1)}, u32[]{:S(2)}) copy-start(bf16[4,1,512,64]{3,2,1,0:T(8,128)(2,1)} %copy-done.3) | copy-start | bytes 786436 | tf_op jit(solution)/shard_map/vmap()/while
  160.3 4.7 %copy-start.7 = (bf16[32,192]{1,0:T(8,128)(2,1)S(1)}, bf16[32,192]{1,0:T(8,128)(2,1)}, u32[]{:S(2)}) copy-start(bf16[32,192]{1,0:T(8,128)(2,1)} %param.11) | copy-start | bytes 36868
  160.3 40.0 %copy-start.5 = (f32[4,1,512,64]{2,0,3,1:T(4,128)S(1)}, f32[4,1,512,64]{2,0,3,1:T(4,128)}, u32[]{:S(2)}) copy-start(f32[4,1,512,64]{2,0,3,1:T(4,128)} %get-tuple-element.71) | copy-start | bytes 1572868
  163.6 37.0 %copy-start.2 = (bf16[128,16,1,192]{0,3,2,1:T(8,128)(2,1)S(1)}, bf16[128,16,1,192]{0,3,2,1:T(8,128)(2,1)}, u32[]{:S(2)}) copy-start(bf16[128,16,1,192]{0,3,2,1:T(8,128)(2,1)} %copy-done.1) | copy-start | bytes 2359300
  164.9 190.3 %all-gather.3.cloned.1.call-start = ((), (), s32[]{:S(2)}) async-start(), calls=%async_computation.4 | async-start | bytes 6684672 | tf_op jit(solution)/shard_map/all_gather | solution.py:155
  202.4 67.9 %all-to-all-start.2 = ((bf16[16,128,192]{1,2,0:T(8,128)(2,1)}), bf16[16,128,192]{1,2,0:T(8,128)(2,1)S(1)}, u32[]{:S(2)}, u32[]{:S(2)}) async-start(bf16[16,128,192]{1,2,0:T(8,128)(2,1)} %copy.98), calls=%async_computation.2 | async-start | bytes 1572864 | tf_op jit(solution)/shard_map/all_to_all | solution.py:152
Sparse Core Ops, SparseCore 0:
  51.7 83.2 all-gather.4
  165.1 103.6 reduce-scatter.3
  270.8 84.3 all-gather.2
where the time goes:
time: 388 us; the launch traced here: 383 us
  waiting for transfers between devices  191 us (49%)
  matrix products  69 us (18%)
  blocking collectives  34.3 us (9%)
  local copies, waits for them, and re-layouts  33.7 us (9%)
  starting transfers between devices  32.5 us (8%)
  between operations  14.1 us (4%)
  other arithmetic  8.59 us (2%)
    all_gather x1, waiting for transfers between devices, body(): piece = lax.all_gather(weight_cols_band, 'ctx', axis=1, tiled=True)  84.9 us
    unnamed x4, waiting for transfers between devices  60.7 us
    all_gather x1, blocking collectives, body(): weight_cols_band = lax.all_gather(w_qkv, 'dp', axis=0, tiled=True)  34.3 us
    all_to_all x1, waiting for transfers between devices, body(): lax.all_to_all(pre_split, 'ctx', split_axis=1, concat_axis=0, tiled=True)  33.6 us
    dot_general x4, matrix products, tile_grads(): lax.dot_general(weights, grad_block, across, preferred_element_type=jnp.f...  20.1 us
    dot_general x16, matrix products, body(): lax.dot_general(part, piece[:, group * columns:(group + 1) * columns], co...  19.8 us
    all_to_all x1, starting transfers between devices, body(): lax.all_to_all(grad_split, 'ctx', split_axis=1, concat_axis=0, tiled=True)  15.7 us
    dynamic_update_slice x8, local copies, waits for them, and re-layouts, dense_grads(): lax.scan(step, (empty, empty), (blocked(query_rows), blocked(grad_rows),...  15.1 us
  transfers between devices with their start and end apart: 6, of which 4 were waited for; matrix products, arithmetic and copies ran while one was open for 21% of the time, Pallas kernels for 0%

commit v1 on v0

v1 whole, which is shorter than its diff:
```python
import functools

import jax
import jax.numpy as jnp
from jax import lax
from jax.experimental import pallas as pl
from jax.experimental.pallas import tpu as pltpu
from jax.sharding import PartitionSpec as P

DH = 64
BLK = 128
MESH = pl.DeviceIdType.MESH
VMEM = pl.BlockSpec(memory_space=pltpu.VMEM)


def attention_kernel(tile, lengths_ref, perm_ref, x_ref, out_ref, q_s, k_s, v_s, g_s, kt_s, gq_s, gk_s, gv_s, start_s, scale_s):
    slots = x_ref.shape[0]
    whole = slots * BLK
    users = lengths_ref.shape[1]
    count = whole // tile

    pos = lax.broadcasted_iota(jnp.int32, (count, tile), 0) * tile + lax.broadcasted_iota(jnp.int32, (count, tile), 1)
    first = jnp.zeros((count, tile), jnp.int32)
    length = jnp.ones((count, tile), jnp.int32)
    end = jnp.int32(0)
    for user in range(users):
        begin = end
        end = begin + lengths_ref[0, user]
        inside = pos >= begin
        first = jnp.where(inside, begin, first)
        length = jnp.where(inside, lengths_ref[0, user], length)
    start_s[...] = first
    scale_s[...] = lax.rsqrt(length.astype(jnp.float32))

    @pl.loop(0, slots)
    def _(slot):
        row = pl.multiple_of(perm_ref[0, slot] * BLK, BLK)
        block = x_ref[slot]
        pre = block[:, : 3 * DH].astype(jnp.float32)
        active = (pre * jax.nn.sigmoid(pre)).astype(jnp.bfloat16)
        q_s[pl.ds(row, BLK), :] = active[:, :DH] * jnp.bfloat16(0.0625)
        key = active[:, DH : 2 * DH]
        k_s[pl.ds(row, BLK), :] = key
        kt_s[:, pl.ds(row, BLK)] = key.T
        v_s[pl.ds(row, BLK), :] = active[:, 2 * DH :]
        g_s[pl.ds(row, BLK), :] = block[:, 3 * DH :]

    gq_s[...] = jnp.zeros_like(gq_s)
    contract = (((1,), (1,)), ((), ()))

    @pl.loop(0, count)
    def _(key_block):
        key_row = pl.multiple_of(key_block * tile, tile)
        last_key = key_row + tile - 1
        limit = jnp.int32(0)
        total = jnp.int32(0)
        for user in range(users):
            begin = total
            total = begin + lengths_ref[0, user]
            limit = jnp.where(last_key >= begin, total, limit)
        stop = (limit + tile - 1) // tile
        keys = k_s[pl.ds(key_row, tile), :]
        values = v_s[pl.ds(key_row, tile), :]
        keys_t = kt_s[:, pl.ds(key_row, tile)]
        key_pos = key_row + lax.broadcasted_iota(jnp.int32, (tile, 1), 0)

        def step(query_block, carry):
            gk, gv = carry
            query_row = pl.multiple_of(query_block * tile, tile)
            queries = q_s[pl.ds(query_row, tile), :]
            grads = g_s[pl.ds(query_row, tile), :]
            half = lax.dot_general(keys, queries, contract, preferred_element_type=jnp.float32)
            gw = lax.dot_general(values, grads, contract, preferred_element_type=jnp.float32)
            first_row = start_s[pl.ds(query_block, 1), :]
            scale_row = scale_s[pl.ds(query_block, 1), :]
            query_pos = query_row + lax.broadcasted_iota(jnp.int32, (1, tile), 1)
            visible = (key_pos >= first_row) & (key_pos <= query_pos)
            th = jnp.tanh(half)
            up = 1.0 + th
            w = half * up
            slope = up + w * (1.0 - th)
            weights = jnp.where(visible, w * scale_row, 0.0).astype(jnp.bfloat16)
            gs = jnp.where(visible, gw * slope * scale_row, 0.0).astype(jnp.bfloat16)
            gv = gv + jnp.dot(weights, grads, preferred_element_type=jnp.float32)
            gk = gk + jnp.dot(gs, queries, preferred_element_type=jnp.float32)
            gq_s[:, pl.ds(query_row, tile)] += jnp.dot(keys_t, gs, preferred_element_type=jnp.float32)
            return gk, gv

        zero = jnp.zeros((tile, DH), jnp.float32)
        gk, gv = lax.fori_loop(key_block, stop, step, (zero, zero))
        gk_s[pl.ds(key_row, tile), :] = gk
        gv_s[pl.ds(key_row, tile), :] = gv

    @pl.loop(0, slots)
    def _(slot):
        row = pl.multiple_of(perm_ref[0, slot] * BLK, BLK)
        pre = x_ref[slot][:, : 3 * DH].astype(jnp.float32)
        sigma = jax.nn.sigmoid(pre)
        slope = sigma * (1.0 + pre * (1.0 - sigma))
        gq = gq_s[:, pl.ds(row, BLK)].T * 0.0625
        gk = gk_s[pl.ds(row, BLK), :]
        gv = gv_s[pl.ds(row, BLK), :]
        out_ref[slot, :DH, :] = (gq * slope[:, :DH]).T.astype(jnp.bfloat16)
        out_ref[slot, DH : 2 * DH, :] = (gk * slope[:, DH : 2 * DH]).T.astype(jnp.bfloat16)
        out_ref[slot, 2 * DH :, :] = (gv * slope[:, 2 * DH :]).T.astype(jnp.bfloat16)


def attention(packed, lengths, perm, tile=256):
    slots = packed.shape[0]
    whole = slots * BLK
    vmem = pl.BlockSpec(memory_space=pltpu.VMEM)
    smem = pl.BlockSpec(memory_space=pltpu.SMEM)
    bf, f32 = jnp.bfloat16, jnp.float32
    return pl.pallas_call(
        functools.partial(attention_kernel, tile),
        out_shape=jax.ShapeDtypeStruct((slots, 3 * DH, BLK), bf),
        in_specs=[smem, smem, vmem],
        out_specs=vmem,
        scratch_shapes=[
            pltpu.VMEM((whole, DH), bf),
            pltpu.VMEM((whole, DH), bf),
            pltpu.VMEM((whole, DH), bf),
            pltpu.VMEM((whole, DH), bf),
            pltpu.VMEM((DH, whole), bf),
            pltpu.VMEM((DH, whole), f32),
            pltpu.VMEM((whole, DH), f32),
            pltpu.VMEM((whole, DH), f32),
            pltpu.VMEM((whole // tile, tile), jnp.int32),
            pltpu.VMEM((whole // tile, tile), f32),
        ],
        compiler_params=pltpu.CompilerParams(vmem_limit_bytes=32 << 20),
    )(lengths, perm, packed)


def exchange_kernel(n, src_ref, dst_ref, send_sem, recv_sem, local_sem):
    me = lax.axis_index("ctx")
    barrier = pltpu.get_barrier_semaphore()
    for step in range(1, n):
        peer = lax.rem(me + step, n)
        pl.semaphore_signal(barrier, inc=1, device_id={"ctx": peer}, device_id_type=MESH)
    own = pltpu.make_async_copy(src_ref.at[me], dst_ref.at[me], local_sem)
    own.start()
    pl.semaphore_wait(barrier, n - 1)
    copies = []
    for near in range(1, n // 2 + 1):
        for step in sorted({near, n - near}):
            peer = lax.rem(me + step, n)
            copy = pltpu.make_async_remote_copy(
                src_ref=src_ref.at[peer],
                dst_ref=dst_ref.at[me],
                send_sem=send_sem.at[step],
                recv_sem=recv_sem.at[step],
                device_id={"ctx": peer},
                device_id_type=MESH,
            )
            copy.start()
            copies.append(copy)
    own.wait()
    for copy in copies:
        copy.wait()


def exchange(blocks, collective_id):
    n = blocks.shape[0]
    return pl.pallas_call(
        functools.partial(exchange_kernel, n),
        out_shape=jax.ShapeDtypeStruct(blocks.shape, blocks.dtype),
        in_specs=[VMEM],
        out_specs=VMEM,
        scratch_shapes=[
            pltpu.SemaphoreType.DMA((n,)),
            pltpu.SemaphoreType.DMA((n,)),
            pltpu.SemaphoreType.DMA,
        ],
        compiler_params=pltpu.CompilerParams(
            collective_id=collective_id, has_side_effects=True, vmem_limit_bytes=16 << 20
        ),
    )(blocks)


def body(layer_input, projected, grad_output, w_qkv, lengths, block_perm):
    tokens_dev = layer_input.shape[1]
    width = layer_input.shape[2]
    ctx_count = lax.axis_size("ctx")
    data_count = lax.axis_size("dp")
    whole = tokens_dev * ctx_count
    columns = 3 * DH
    packed = jnp.concatenate(
        [
            projected[0].reshape(tokens_dev, ctx_count, columns),
            grad_output[0].reshape(tokens_dev, ctx_count, DH),
        ],
        axis=2,
    ).transpose(1, 0, 2)
    grad_t = attention(exchange(packed, 1), lengths, block_perm)
    tokens = lax.all_gather(layer_input, "ctx", axis=1, tiled=True)[0]
    flat_t = grad_t.transpose(1, 0, 2).reshape(columns, whole)
    weight_local = lax.dot_general(
        tokens, flat_t, (((0,), (1,)), ((), ())), preferred_element_type=jnp.float32
    )
    grad_weight = lax.psum_scatter(weight_local, "dp", scatter_dimension=0, tiled=True) * (
        1.0 / data_count
    )
    back_t = exchange(grad_t, 2).reshape(ctx_count * columns, tokens_dev)
    w_rows = lax.all_gather(w_qkv, "ctx", axis=1, tiled=True)
    w_all = lax.all_gather(w_rows, "dp", axis=0, tiled=True)
    grad_input = lax.dot_general(
        back_t, w_all, (((0,), (1,)), ((), ())), preferred_element_type=jnp.float32
    ).astype(jnp.bfloat16)
    return (grad_input[None], grad_weight)


def solution(mesh):
    return jax.shard_map(
        body,
        mesh=mesh,
        in_specs=(
            P("dp", "ctx", None),
            P("dp", "ctx", None),
            P("dp", "ctx", None),
            P("dp", "ctx"),
            P("dp", None),
            P("dp", None),
        ),
        out_specs=(P("dp", "ctx", None), P("dp", "ctx")),
        check_vma=False,
    )
```

time: 388 us -> 308 us (0.79); the launches traced: 383 us -> 308 us
  Pallas kernels: 0 us -> 110 us
  matrix products: 69 us -> 8.87 us
  waiting for transfers between devices: 191 us -> 145 us
  starting transfers between devices: 32.5 us -> 0.12 us
  local copies, waits for them, and re-layouts: 33.7 us -> 7.4 us
  blocking collectives: 34.3 us -> 22.6 us
  other arithmetic: 8.59 us -> 0.34 us
    pallas_call x0 -> x3, Pallas kernels: none -> 110 us  [the longest x2 93.6 us: exchange(): pl.pallas_call(functools.partial(exchange_kernel, n), out_shape=jax.Shape...]
    dot_general x37 -> x2, matrix products: 69 us -> 8.87 us  [the longest x1 5.71 us: body(): lax.dot_general(back_t, w_all, (((0,), (1,)), ((), ())), preferred_elemen...]
    all_to_all x3 -> x0, waiting for transfers between devices: 45.1 us -> none  [the longest x1 33.6 us: body(): lax.all_to_all(pre_split, 'ctx', split_axis=1, concat_axis=0, tiled=True)]
    all_to_all x3 -> x0, starting transfers between devices: 32.4 us -> none  [the longest x1 15.7 us: body(): lax.all_to_all(grad_split, 'ctx', split_axis=1, concat_axis=0, tiled=True)]
    dynamic_update_slice x8 -> x0, local copies, waits for them, and re-layouts: 15.1 us -> none  [dense_grads(): lax.scan(step, (empty, empty), (blocked(query_rows), blocked(grad_rows),...]
    unnamed x4, waiting for transfers between devices: 60.7 us -> 48.9 us
    all_gather x1, blocking collectives: 34.3 us -> 22.6 us  [body(): w_rows = lax.all_gather(w_qkv, 'ctx', axis=1, tiled=True)]
    all_gather x2, waiting for transfers between devices: 85 us -> 96.1 us  [the longest x1 68.2 us: body(): w_all = lax.all_gather(w_rows, 'dp', axis=0, tiled=True)]
  transfers between devices with their start and end apart: 6 -> 3, of which waited for: 4 -> 3; matrix products, arithmetic and copies ran while one was open for 21% -> 2% of each run, Pallas kernels for 0% -> 36%
where the time goes in v1:
time: 308 us
  waiting for transfers between devices  145 us (47%)
  Pallas kernels  110 us (36%)
  blocking collectives  22.6 us (7%)
  between operations  13.9 us (5%)
  matrix products  8.87 us (3%)
  local copies, waits for them, and re-layouts  7.4 us (2%)
    pallas_call x2, Pallas kernels, exchange(): pl.pallas_call(functools.partial(exchange_kernel, n), out_shape=jax.Shape...  93.6 us
    all_gather x1, waiting for transfers between devices, body(): w_all = lax.all_gather(w_rows, 'dp', axis=0, tiled=True)  68.2 us
    unnamed x4, waiting for transfers between devices  48.9 us
    all_gather x1, waiting for transfers between devices, body(): tokens = lax.all_gather(layer_input, 'ctx', axis=1, tiled=True)[0]  27.9 us
    all_gather x1, blocking collectives, body(): w_rows = lax.all_gather(w_qkv, 'ctx', axis=1, tiled=True)  22.6 us
    pallas_call x1, Pallas kernels, attention(): pl.pallas_call(functools.partial(attention_kernel, tile), out_shape=jax.S...  15.9 us
    unnamed x12, local copies, waits for them, and re-layouts  6.45 us
  transfers between devices with their start and end apart: 3, of which 3 were waited for; matrix products, arithmetic and copies ran while one was open for 2% of the time, Pallas kernels for 36%

profile of v1, /device:TPU:1, one launch (start us, length us, event | category | flops | bytes accessed | tf_op | source)
XLA Modules:
  0.0 307.8 jit_solution(3796437875536679569)
XLA Ops:
  7.2 0.0 all-gather.6.cloned.1.call-start
  7.2 0.7 all-gather.6.cloned.1.call-update
  7.9 0.0 reduce-scatter.4.cloned.1.call-start
  7.9 1.5 copy.16
  9.5 0.0 copy-start
  9.5 0.0 copy-start.1
  9.5 0.5 copy.18
  10.0 1.1 copy.17
  11.1 0.3 copy.19
  11.4 0.3 maximum_bitcast_fusion.src_ref
  11.8 63.9 %shard_map.77.x_ref = bf16[16,128,256]{2,1,0:T(8,128)(2,1)S(1)} custom-call(bf16[16,128,256]{2,1,0:T(8,128)(2,1)S(1)} %maximum_bitcast_fusion.src_ref), custom_call_target="tpu_custom_call" | custom-call | tf_op jit(solution)/shard_map/pallas_call | solution.py:165
  75.7 0.0 copy-done
  75.7 0.0 copy-done.1
  75.7 15.9 %shard_map.78.src_ref = bf16[16,192,128]{2,1,0:T(8,128)(2,1)S(1)} custom-call(s32[1,8]{1,0:T(1,128)S(1)} %copy-done, s32[1,16]{1,0:T(1,128)S(1)} %copy-done.1, bf16[16,128,256]{2,1,0:T(8,128)(2,1)S(1)} %shard_map.77.x_ref), custom_call_target="tpu_custom_call" | custom-call | tf_op jit(solution)/shard_map/pallas_call | solution.py:114
  91.7 0.0 copy-start.2
  91.7 27.9 %all-gather.6.cloned.1.call-done = bf16[1,2048,1024]{2,1,0:T(8,128)(2,1)} async-done(((bf16[1,128,1024]{2,1,0:T(8,128)(2,1)}), bf16[1,2048,1024]{2,1,0:T(8,128)(2,1)}) %all-gather.6.cloned.1.call-update) | async-done | bytes 4194320 | tf_op jit(solution)/shard_map/all_gather | solution.py:196
  119.6 3.2 %fusion.2 = f32[1024,192]{0,1:T(8,128)S(1)} fusion(bf16[1,2048,1024]{2,1,0:T(8,128)(2,1)} %all-gather.6.cloned.1.call-done, bf16[16,192,128]{2,1,0:T(8,128)(2,1)S(1)} %shard_map.78.src_ref), kind=kOutput, calls=%fused_computation.2 | convolution fusion | flops 805306368 | bytes 5767168 | tf_op jit(solution)/shard_map/dot_general | solution.py:198
  122.8 1.3 copy.23
  124.1 0.0 reduce-scatter.4.cloned.1.call-update
  124.2 0.0 all-gather.4.cloned.1.call-start
  124.2 0.0 copy-done.2
  124.2 22.6 %all-gather = bf16[16,192,32]{1,2,0:T(8,128)(2,1)S(1)} all-gather(bf16[1,192,32]{1,2,0:T(8,128)(2,1)S(1)} %bitcast.35), channel_id=1, replica_groups=mesh['dp'=32,'ctx'=16] {'ctx'}, dimensions={0}, use_global_device_ids=true | all-gather | bytes 208896 | tf_op jit(solution)/shard_map/all_gather | solution.py:205
  146.9 0.1 copy.20
  147.0 0.9 reshape.13
  148.0 0.0 all-gather.4.cloned.1.call-update
  148.0 29.6 %shard_map.79 = bf16[16,192,128]{2,1,0:T(8,128)(2,1)S(1)} custom-call(bf16[16,192,128]{2,1,0:T(8,128)(2,1)S(1)} %shard_map.78.src_ref), custom_call_target="tpu_custom_call" | custom-call | tf_op jit(solution)/shard_map/pallas_call | solution.py:165
  177.6 48.2 %reduce-scatter.4.cloned.1.call-done = f32[32,192]{1,0:T(8,128)} async-done(((f32[1024,192]{1,0:T(8,128)}), f32[32,192]{1,0:T(8,128)}) %reduce-scatter.4.cloned.1.call-update) | async-done | bytes 24592
  225.8 0.9 copy.24
  226.7 0.7 copy.22
  227.4 68.2 %all-gather.4.cloned.1.call-done = bf16[1024,3072]{1,0:T(8,128)(2,1)} async-done(((bf16[32,3072]{1,0:T(8,128)(2,1)}), bf16[1024,3072]{1,0:T(8,128)(2,1)}) %all-gather.4.cloned.1.call-update) | async-done | bytes 6291472 | tf_op jit(solution)/shard_map/all_gather | solution.py:206
  295.6 5.7 %fusion.5 = bf16[1,128,1024]{2,1,0:T(8,128)(2,1)} fusion(bf16[3072,128]{1,0:T(8,128)(2,1)S(1)} %bitcast.31, bf16[1024,3072]{1,0:T(8,128)(2,1)} %all-gather.4.cloned.1.call-done), kind=kOutput, calls=%fused_computation.4 | convolution fusion | flops 805437440 | bytes 7340032 | tf_op jit(solution)/shard_map/dot_general | solution.py:207
  (1 shorter events, 0.0 us)
Async XLA Ops:
  7.2 112.5 %all-gather.6.cloned.1.call-start = ((), (), s32[]{:S(2)}) async-start(), calls=%async_computation.2 | async-start | bytes 4456448 | tf_op jit(solution)/shard_map/all_gather | solution.py:196
  7.9 217.9 %reduce-scatter.4.cloned.1.call-start = ((), (), s32[]{:S(2)}) async-start(), calls=%async_computation.3 | async-start | bytes 1081344
  9.5 66.3 %copy-start = (s32[1,8]{1,0:T(1,128)S(1)}, s32[1,8]{1,0:T(1,128)}, u32[]{:S(2)}) copy-start(s32[1,8]{1,0:T(1,128)} %lengths_ref.1) | copy-start | bytes 100
  9.5 66.3 %copy-start.1 = (s32[1,16]{1,0:T(1,128)S(1)}, s32[1,16]{1,0:T(1,128)}, u32[]{:S(2)}) copy-start(s32[1,16]{1,0:T(1,128)} %perm_ref.1) | copy-start | bytes 196
  91.7 32.5 %copy-start.2 = (bf16[32,192]{1,0:T(8,128)(2,1)S(1)}, bf16[32,192]{1,0:T(8,128)(2,1)}, u32[]{:S(2)}) copy-start(bf16[32,192]{1,0:T(8,128)(2,1)} %param.9) | copy-start | bytes 36868
  124.2 171.4 %all-gather.4.cloned.1.call-start = ((), (), s32[]{:S(2)}) async-start(), calls=%async_computation.1 | async-start | bytes 6488064 | tf_op jit(solution)/shard_map/all_gather | solution.py:206
Sparse Core Ops, SparseCore 0:
  10.0 109.5 all-gather.5
  124.3 101.5 reduce-scatter.3
  229.5 65.9 all-gather.3

commit v2 on v1

--- a/solution.py
+++ b/solution.py
@@ -11,6 +11,7 @@
 BLK = 128
 MESH = pl.DeviceIdType.MESH
 VMEM = pl.BlockSpec(memory_space=pltpu.VMEM)
+ANY = pl.BlockSpec(memory_space=pl.ANY)
 
 
 def attention_kernel(tile, lengths_ref, perm_ref, x_ref, out_ref, q_s, k_s, v_s, g_s, kt_s, gq_s, gk_s, gv_s, start_s, scale_s):
@@ -132,50 +133,317 @@
     )(lengths, perm, packed)
 
 
-def exchange_kernel(n, src_ref, dst_ref, send_sem, recv_sem, local_sem):
+class Links:
+    def __init__(self, send_sem, recv_sem):
+        self.send_sem, self.recv_sem = send_sem, recv_sem
+        self.copies = []
+
+    def start(self, src, dst, device):
+        k = len(self.copies)
+        copy = pltpu.make_async_remote_copy(
+            src_ref=src,
+            dst_ref=dst,
+            send_sem=self.send_sem.at[k],
+            recv_sem=self.recv_sem.at[k],
+            device_id=device,
+            device_id_type=MESH,
+        )
+        copy.start()
+        self.copies.append(copy)
+        return copy
+
+    def wait_sends(self):
+        for copy in self.copies:
+            copy.wait_send()
+
+
+def far_first(n):
+    order = []
+    for near in range(n // 2, 0, -1):
+        order += sorted({near, n - near})
+    return order
+
+
+def all_to_all_start(links, axis, me, n, src_ref, dst_ref):
+    copies = []
+    for step in far_first(n):
+        peer = lax.rem(me + step, n)
+        copies.append(links.start(src_ref.at[peer], dst_ref.at[me], {axis: peer}))
+    return copies
+
+
+def ring_gather(links, me, n, own_ref, all_ref):
+    rows = own_ref.shape[0] // 2
+    right, left = {"ctx": lax.rem(me + 1, n)}, {"ctx": lax.rem(me + n - 1, n)}
+    part = [pl.ds(0, rows), pl.ds(rows, rows)]
+    far = n // 2
+    ahead, back = {}, {}
+    for half in range(2):
+        ahead[1, half] = links.start(own_ref.at[part[half]], all_ref.at[me, part[half]], right)
+        back[1, half] = links.start(own_ref.at[part[half]], all_ref.at[me, part[half]], left)
+    for step in range(1, far):
+        below, above = lax.rem(me + n - step, n), lax.rem(me + step, n)
+        yield
+        for half in range(2):
+            ahead[step, half].wait_recv()
+            if step < far - 1 or half == 0:
+                ref = all_ref.at[below, part[half]]
+                ahead[step + 1, half] = links.start(ref, ref, right)
+            back[step, half].wait_recv()
+            if step < far - 1 or half == 1:
+                ref = all_ref.at[above, part[half]]
+                back[step + 1, half] = links.start(ref, ref, left)
+    yield
+    ahead[far, 0].wait_recv()
+    back[far, 1].wait_recv()
+
+
+def plane_gather(links, own_ref, all_ref, side=4):
+    dp = lax.axis_index("dp")
+    core = lax.rem(dp, 2)
+    chip = lax.div(dp, 2)
+    x, y = lax.rem(chip, side), lax.div(chip, side)
+    a = x * (1 - core) + y * core
+    b = y * (1 - core) + x * core
+    partner = {"dp": dp + 1 - 2 * core}
+    depth = own_ref.shape[0] // 2
+    part = [pl.ds(0, depth), pl.ds(depth, depth)]
+
+    def index(i, j):
+        p, q = lax.rem(a + i + side, side), lax.rem(b + j + side, side)
+        px = p * (1 - core) + q * core
+        py = q * (1 - core) + p * core
+        return (py * side + px) * 2 + core
+
+    def device(i, j):
+        return {"dp": index(i, j)}
+
+    across = []
+
+    def hand_over(i, j, src=None):
+        ref = all_ref.at[index(i, j)]
+        across.append(links.start(ref if src is None else src, ref, partner))
+
+    def spread(i, src=None):
+        ref = all_ref.at[index(i, 0)]
+        src = ref if src is None else src
+        up = links.start(src, ref, device(0, 1))
+        down = links.start(src, ref, device(0, -1))
+        hand_over(i, 0, src)
+        return up, down
+
+    def pass_on(i, pair):
+        up, down = pair
+        up.wait_recv()
+        ref = all_ref.at[index(i, -1), part[1]]
+        far_up = links.start(ref, ref, device(0, 1))
+        hand_over(i, -1)
+        down.wait_recv()
+        ref = all_ref.at[index(i, 1), part[0]]
+        far_down = links.start(ref, ref, device(0, -1))
+        hand_over(i, 1)
+        return far_up, far_down
+
+    def finish(i, pair):
+        pair[0].wait_recv()
+        pair[1].wait_recv()
+        hand_over(i, 2)
+
+    own_slot = all_ref.at[index(0, 0)]
+    up = links.start(own_ref, own_slot, device(1, 0))
+    down = links.start(own_ref, own_slot, device(-1, 0))
+    first = spread(0, own_ref)
+    yield
+    up.wait_recv()
+    ref = all_ref.at[index(-1, 0), part[1]]
+    far_up = links.start(ref, ref, device(1, 0))
+    second = spread(-1)
+    yield
+    down.wait_recv()
+    ref = all_ref.at[index(1, 0), part[0]]
+    far_down = links.start(ref, ref, device(-1, 0))
+    third = spread(1)
+    yield
+    first = pass_on(0, first)
+    yield
+    far_up.wait_recv()
+    far_down.wait_recv()
+    fourth = spread(2)
+    yield
+    second = pass_on(-1, second)
+    yield
+    third = pass_on(1, third)
+    yield
+    finish(0, first)
+    fourth = pass_on(2, fourth)
+    yield
+    finish(-1, second)
+    finish(1, third)
+    yield
+    finish(2, fourth)
+    yield
+    for copy in across:
+        copy.wait_recv()
+
+
+PLANE_COPIES = 2 + 2 + 4 * 4 + 16
+
+
+def greet(axis_peers):
+    barrier = pltpu.get_barrier_semaphore()
+    for device in axis_peers:
+        pl.semaphore_signal(barrier, inc=1, device_id=device, device_id_type=MESH)
+    return barrier, len(axis_peers)
+
+
+def gather_kernel(n, packed_ref, tokens_ref, w_ref, recv_ref, tokens_all_ref, w_all_ref, w_rows, send_sem, recv_sem, local_sem):
     me = lax.axis_index("ctx")
-    barrier = pltpu.get_barrier_semaphore()
-    for step in range(1, n):
-        peer = lax.rem(me + step, n)
-        pl.semaphore_signal(barrier, inc=1, device_id={"ctx": peer}, device_id_type=MESH)
-    own = pltpu.make_async_copy(src_ref.at[me], dst_ref.at[me], local_sem)
-    own.start()
-    pl.semaphore_wait(barrier, n - 1)
-    copies = []
-    for near in range(1, n // 2 + 1):
-        for step in sorted({near, n - near}):
-            peer = lax.rem(me + step, n)
-            copy = pltpu.make_async_remote_copy(
-                src_ref=src_ref.at[peer],
-                dst_ref=dst_ref.at[me],
-                send_sem=send_sem.at[step],
-                recv_sem=recv_sem.at[step],
-                device_id={"ctx": peer},
-                device_id_type=MESH,
-            )
-            copy.start()
-            copies.append(copy)
-    own.wait()
+    dp = lax.axis_index("dp")
+    core = lax.rem(dp, 2)
+    chip = lax.div(dp, 2)
+    x, y = lax.rem(chip, 4), lax.div(chip, 4)
+    peers = [{"ctx": lax.rem(me + step, n)} for step in range(1, n)]
+    peers += [{"dp": dp + 1 - 2 * core}]
+    peers += [{"dp": (y * 4 + lax.rem(x + step, 4)) * 2 + core} for step in (1, 3)]
+    peers += [{"dp": (lax.rem(y + step, 4) * 4 + x) * 2 + core} for step in (1, 3)]
+    barrier, count = greet(peers)
+    links = Links(send_sem, recv_sem)
+    own_w = pltpu.make_async_copy(w_ref, w_rows.at[me], local_sem.at[0])
+    own_w.start()
+    own_block = pltpu.make_async_copy(packed_ref.at[me], recv_ref.at[me], local_sem.at[1])
+    own_block.start()
+    own_tokens = pltpu.make_async_copy(tokens_ref, tokens_all_ref.at[me], local_sem.at[2])
+    own_tokens.start()
+    pl.semaphore_wait(barrier, count)
+    rows_in = []
+    for step in far_first(n):
+        rows_in.append(links.start(w_ref, w_rows.at[me], {"ctx": lax.rem(me + step, n)}))
+    ring = ring_gather(links, me, n, tokens_ref, tokens_all_ref)
+    next(ring)
+    blocks_in = all_to_all_start(links, "ctx", me, n, packed_ref, recv_ref)
+    own_w.wait()
+    for copy in rows_in:
+        copy.wait_recv()
+    own_rows = pltpu.make_async_copy(w_rows, w_all_ref.at[dp], local_sem.at[0])
+    own_rows.start()
+    plane = plane_gather(links, w_rows, w_all_ref)
+    going = [plane, ring]
+    while going:
+        for chain in list(going):
+            try:
+                next(chain)
+            except StopIteration:
+                going.remove(chain)
+    for copy in blocks_in:
+        copy.wait_recv()
+    links.wait_sends()
+    own_rows.wait()
+    own_block.wait()
+    own_tokens.wait()
+
+
+def gather(packed, tokens, w, planes):
+    n = packed.shape[0]
+    copies = (n - 1) * 2 + 2 * (n - 1) + PLANE_COPIES
+    return pl.pallas_call(
+        functools.partial(gather_kernel, n),
+        out_shape=(
+            jax.ShapeDtypeStruct(packed.shape, packed.dtype),
+            jax.ShapeDtypeStruct((n,) + tokens.shape, tokens.dtype),
+            jax.ShapeDtypeStruct((planes, n) + w.shape, w.dtype),
+        ),
+        in_specs=[VMEM, VMEM, VMEM],
+        out_specs=(VMEM, ANY, ANY),
+        scratch_shapes=[
+            pltpu.VMEM((n,) + w.shape, w.dtype),
+            pltpu.SemaphoreType.DMA((copies,)),
+            pltpu.SemaphoreType.DMA((copies,)),
+            pltpu.SemaphoreType.DMA((3,)),
+        ],
+        compiler_params=pltpu.CompilerParams(
+            collective_id=1, has_side_effects=True, vmem_limit_bytes=16 << 20
+        ),
+    )(packed, tokens, w)
+
+
+def return_kernel(n, planes, grad_ref, part_ref, back_ref, parts_ref, send_sem, recv_sem, local_sem):
+    me = lax.axis_index("ctx")
+    dp = lax.axis_index("dp")
+    peers = [{"ctx": lax.rem(me + step, n)} for step in range(1, n)]
+    peers += [{"dp": lax.rem(dp + step, planes)} for step in range(1, planes)]
+    barrier, count = greet(peers)
+    own_block = pltpu.make_async_copy(grad_ref.at[me], back_ref.at[me], local_sem.at[0])
+    own_block.start()
+    own_part = pltpu.make_async_copy(part_ref.at[dp], parts_ref.at[dp], local_sem.at[1])
+    own_part.start()
+    pl.semaphore_wait(barrier, count)
+    links = Links(send_sem, recv_sem)
+    copies = all_to_all_start(links, "ctx", me, n, grad_ref, back_ref)
+    copies += all_to_all_start(links, "dp", dp, planes, part_ref, parts_ref)
+    own_block.wait()
+    own_part.wait()
     for copy in copies:
         copy.wait()
 
 
-def exchange(blocks, collective_id):
-    n = blocks.shape[0]
+def send_back(grad_t, parts):
+    n, planes = grad_t.shape[0], parts.shape[0]
+    copies = n + planes - 2
     return pl.pallas_call(
-        functools.partial(exchange_kernel, n),
-        out_shape=jax.ShapeDtypeStruct(blocks.shape, blocks.dtype),
-        in_specs=[VMEM],
-        out_specs=VMEM,
+        functools.partial(return_kernel, n, planes),
+        out_shape=(
+            jax.ShapeDtypeStruct(grad_t.shape, grad_t.dtype),
+            jax.ShapeDtypeStruct(parts.shape, parts.dtype),
+        ),
+        in_specs=[VMEM, VMEM],
+        out_specs=(VMEM, VMEM),
         scratch_shapes=[
-            pltpu.SemaphoreType.DMA((n,)),
-            pltpu.SemaphoreType.DMA((n,)),
-            pltpu.SemaphoreType.DMA,
+            pltpu.SemaphoreType.DMA((copies,)),
+            pltpu.SemaphoreType.DMA((copies,)),
+            pltpu.SemaphoreType.DMA((2,)),
         ],
         compiler_params=pltpu.CompilerParams(
-            collective_id=collective_id, has_side_effects=True, vmem_limit_bytes=16 << 20
+            collective_id=2, has_side_effects=True, vmem_limit_bytes=16 << 20
         ),
-    )(blocks)
+    )(grad_t, parts)
+
+
+def input_grad_kernel(back_ref, w_ref, out_ref, total):
+    step = pl.program_id(0)
+    planes, group, rows, columns = w_ref.shape
+    block = w_ref[:, 0].reshape(planes * rows, columns)
+    term = jnp.dot(block, back_ref[0], preferred_element_type=jnp.float32)
+    term = term.astype(jnp.bfloat16).astype(jnp.float32)
+
+    @pl.when(step == 0)
+    def _():
+        total[...] = term
+
+    @pl.when(step > 0)
+    def _():
+        total[...] += term
+
+    @pl.when(step == pl.num_programs(0) - 1)
+    def _():
+        out_ref[...] = total[...].T.astype(out_ref.dtype)
+
+
+def input_grad(back_t, w_all):
+    n, columns, tokens = back_t.shape
+    planes, _, rows, _ = w_all.shape
+    width = planes * rows
+    return pl.pallas_call(
+        input_grad_kernel,
+        grid=(n,),
+        out_shape=jax.ShapeDtypeStruct((tokens, width), jnp.bfloat16),
+        in_specs=[
+            pl.BlockSpec((1, columns, tokens), lambda i: (i, 0, 0)),
+            pl.BlockSpec((planes, 1, rows, columns), lambda i: (0, i, 0, 0)),
+        ],
+        out_specs=pl.BlockSpec((tokens, width), lambda i: (0, 0)),
+        scratch_shapes=[pltpu.VMEM((width, tokens), jnp.float32)],
+        compiler_params=pltpu.CompilerParams(dimension_semantics=("arbitrary",)),
+    )(back_t, w_all)
 
 
 def body(layer_input, projected, grad_output, w_qkv, lengths, block_perm):
@@ -183,7 +451,6 @@
     width = layer_input.shape[2]
     ctx_count = lax.axis_size("ctx")
     data_count = lax.axis_size("dp")
-    whole = tokens_dev * ctx_count
     columns = 3 * DH
     packed = jnp.concatenate(
         [
@@ -192,22 +459,18 @@
         ],
         axis=2,
     ).transpose(1, 0, 2)
-    grad_t = attention(exchange(packed, 1), lengths, block_perm)
-    tokens = lax.all_gather(layer_input, "ctx", axis=1, tiled=True)[0]
-    flat_t = grad_t.transpose(1, 0, 2).reshape(columns, whole)
+    blocks, tokens_all, w_all = gather(packed, layer_input[0], w_qkv, data_count)
+    grad_t = attention(blocks, lengths, block_perm)
     weight_local = lax.dot_general(
-        tokens, flat_t, (((0,), (1,)), ((), ())), preferred_element_type=jnp.float32
+        tokens_all.reshape(ctx_count * tokens_dev, width),
+        grad_t.transpose(1, 0, 2).reshape(columns, ctx_count * tokens_dev),
+        (((0,), (1,)), ((), ())),
+        preferred_element_type=jnp.float32,
     )
-    grad_weight = lax.psum_scatter(weight_local, "dp", scatter_dimension=0, tiled=True) * (
-        1.0 / data_count
-    )
-    back_t = exchange(grad_t, 2).reshape(ctx_count * columns, tokens_dev)
-    w_rows = lax.all_gather(w_qkv, "ctx", axis=1, tiled=True)
-    w_all = lax.all_gather(w_rows, "dp", axis=0, tiled=True)
-    grad_input = lax.dot_general(
-        back_t, w_all, (((0,), (1,)), ((), ())), preferred_element_type=jnp.float32
-    ).astype(jnp.bfloat16)
-    return (grad_input[None], grad_weight)
+    parts = weight_local.reshape(data_count, width // data_count, columns)
+    back_t, parts = send_back(grad_t, parts)
+    grad_weight = jnp.sum(parts, axis=0) * (1.0 / data_count)
+    return (input_grad(back_t, w_all)[None], grad_weight)
 
 
 def solution(mesh):

time: 308 us -> 216 us (0.70)
  waiting for transfers between devices: 145 us -> 0 us
  Pallas kernels: 110 us -> 193 us
  blocking collectives: 22.6 us -> 0 us
  between operations: 13.9 us -> 0.77 us
  local copies, waits for them, and re-layouts: 7.4 us -> 16.9 us
  matrix products: 8.87 us -> 3.46 us
    all_gather x2 -> x0, waiting for transfers between devices: 96.1 us -> none  [the longest x1 68.2 us: body(): w_all = lax.all_gather(w_rows, 'dp', axis=0, tiled=True)]
    pallas_call x2 -> x3, Pallas kernels: 93.6 us -> 178 us  [the longest x1 122 us: gather(): pl.pallas_call(functools.partial(gather_kernel, n), out_shape=(jax.ShapeD...]
    unnamed x4 -> x0, waiting for transfers between devices: 48.9 us -> none
    all_gather x1 -> x0, blocking collectives: 22.6 us -> none  [body(): w_rows = lax.all_gather(w_qkv, 'ctx', axis=1, tiled=True)]
    dot_general x0 -> x1, local copies, waits for them, and re-layouts: none -> 6.47 us  [body(): lax.dot_general(tokens_all.reshape(ctx_count * tokens_dev, width), grad_t...]
    dot_general x2 -> x1, matrix products: 8.87 us -> 3.46 us  [body(): lax.dot_general(tokens_all.reshape(ctx_count * tokens_dev, width), grad_t...]
    unnamed x12 -> x16, local copies, waits for them, and re-layouts: 6.45 us -> 8.81 us
  transfers between devices with their start and end apart: 3 -> 0, of which waited for: 3 -> 0; matrix products, arithmetic and copies ran while one was open for 2% -> 0% of each run, Pallas kernels for 36% -> 0%
where the time goes in v2:
time: 216 us; the launch traced here: 215 us
  Pallas kernels  193 us (89%)
  local copies, waits for them, and re-layouts  16.9 us (8%)
  matrix products  3.46 us (2%)
    pallas_call x1, Pallas kernels, gather(): pl.pallas_call(functools.partial(gather_kernel, n), out_shape=(jax.ShapeD...  122 us
    pallas_call x1, Pallas kernels, send_back(): pl.pallas_call(functools.partial(return_kernel, n, planes), out_shape=(ja...  42.9 us
    pallas_call x1, Pallas kernels, attention(): pl.pallas_call(functools.partial(attention_kernel, tile), out_shape=jax.S...  15.5 us
    pallas_call x1, Pallas kernels, input_grad(): pl.pallas_call(input_grad_kernel, grid=(n,), out_shape=jax.ShapeDtypeStru...  12.8 us
    unnamed x16, local copies, waits for them, and re-layouts  8.81 us
    dot_general x1, local copies, waits for them, and re-layouts, body(): lax.dot_general(tokens_all.reshape(ctx_count * tokens_dev, width), grad_t...  6.47 us

profile of v2, /device:TPU:1, one launch (start us, length us, event | category | flops | bytes accessed | tf_op | source)
XLA Modules:
  0.0 215.4 jit_solution(12027826300666674847)
XLA Ops:
  0.6 0.0 copy-start.4
  0.6 0.0 copy-start.3
  0.6 1.2 copy.10
  1.8 0.0 copy-start.5
  1.8 0.0 copy-start.6
  1.8 0.3 copy.12
  2.1 1.5 copy.9
  3.6 0.5 copy.11
  4.2 0.3 maximum_bitcast_fusion.packed_ref
  4.5 0.0 copy-done.4
  4.5 0.0 copy-done.3
  4.5 122.0 %shard_map.77 = (bf16[16,128,256]{2,1,0:T(8,128)(2,1)S(1)}, bf16[16,128,1024]{2,1,0:T(8,128)(2,1)S(1)}, bf16[32,16,32,192]{3,2,1,0:T(8,128)(2,1)S(1)}) custom-call(bf16[16,128,256]{2,1,0:T(8,128)(2,1)S(1)} %maximum_bitcast_fusion.packed_ref, bf16[128,1024]{1,0:T(8,128)(2,1)S(1)} %bitcast.15, bf16[32,192]{1,0:T(8,128)(2,1)S(1)} %copy-done.4), custom_call_target="tpu_custom_call" | custom-call | tf_op jit(solution)/shard_map/pallas_call | solution.py:348
  126.5 0.0 copy-start
  126.5 3.2 %copy-done = bf16[32,16,32,192]{3,2,1,0:T(8,128)(2,1)} copy-done((bf16[32,16,32,192]{3,2,1,0:T(8,128)(2,1)}, bf16[32,16,32,192]{3,2,1,0:T(8,128)(2,1)S(1)}, u32[]{:S(2)}) %copy-start) | copy-done | bytes 6291480
  129.8 0.0 copy-start.1
  129.8 2.0 copy-done.1
  131.7 0.0 copy-done.5
  131.7 0.0 copy-done.6
  131.7 15.5 %shard_map.78.grad_ref = bf16[16,192,128]{2,1,0:T(8,128)(2,1)S(1)} custom-call(s32[1,8]{1,0:T(1,128)S(1)} %copy-done.5, s32[1,16]{1,0:T(1,128)S(1)} %copy-done.6, bf16[16,128,256]{2,1,0:T(8,128)(2,1)S(1)} %get-tuple-element.7.x_ref), custom_call_target="tpu_custom_call" | custom-call | tf_op jit(solution)/shard_map/pallas_call | solution.py:115
  147.3 6.5 %copy.13 = bf16[1024,2048]{1,0:T(8,128)(2,1)} copy(bf16[1024,2048]{0,1:T(8,128)(2,1)} %bitcast.14) | data formatting | bytes 8388608 | tf_op jit(solution)/shard_map/dot_general | solution.py:464
  153.7 0.5 copy.14
  154.2 0.3 reshape.14
  154.6 3.5 %fusion.part_ref = f32[32,32,192]{2,1,0:T(8,128)S(1)} fusion(bf16[32,32,2048]{2,1,0:T(8,128)(2,1)} %bitcast.16, bf16[192,2048,1]{1,0,2:T(8,128)(2,1)S(1)} %reshape.14), kind=kOutput, calls=%fused_computation.2 | convolution fusion | flops 805306368 | bytes 5767168 | tf_op jit(solution)/shard_map/dot_general | solution.py:464
  158.0 42.9 %shard_map.79 = (bf16[16,192,128]{2,1,0:T(8,128)(2,1)S(1)}, f32[32,32,192]{2,1,0:T(8,128)S(1)}) custom-call(bf16[16,192,128]{2,1,0:T(8,128)(2,1)S(1)} %shard_map.78.grad_ref, f32[32,32,192]{2,1,0:T(8,128)S(1)} %fusion.part_ref), custom_call_target="tpu_custom_call" | custom-call | tf_op jit(solution)/shard_map/pallas_call | solution.py:392
  201.0 0.0 copy-start.2
  201.0 0.9 copy-done.2
  201.9 12.8 %shard_map.80 = bf16[128,1024]{1,0:T(8,128)(2,1)} custom-call(bf16[16,192,128]{2,1,0:T(8,128)(2,1)} %copy-done.2, bf16[32,16,32,192]{3,2,1,0:T(8,128)(2,1)} %copy-done), custom_call_target="tpu_custom_call" | custom-call | tf_op jit(solution)/shard_map/pallas_call | solution.py:435
  214.7 0.1 reduce_sum.9
  214.8 0.6 broadcast_multiply_fusion
Async XLA Ops:
  0.6 3.9 %copy-start.4 = (bf16[32,192]{1,0:T(8,128)(2,1)S(1)}, bf16[32,192]{1,0:T(8,128)(2,1)}, u32[]{:S(2)}) copy-start(bf16[32,192]{1,0:T(8,128)(2,1)} %w_ref.1) | copy-start | bytes 36868
  0.6 3.9 %copy-start.3 = (bf16[1,128,1024]{2,1,0:T(8,128)(2,1)S(1)}, bf16[1,128,1024]{2,1,0:T(8,128)(2,1)}, u32[]{:S(2)}) copy-start(bf16[1,128,1024]{2,1,0:T(8,128)(2,1)} %param.6) | copy-start | bytes 786436
  1.8 129.9 %copy-start.5 = (s32[1,8]{1,0:T(1,128)S(1)}, s32[1,8]{1,0:T(1,128)}, u32[]{:S(2)}) copy-start(s32[1,8]{1,0:T(1,128)} %lengths_ref.1) | copy-start | bytes 100
  1.8 129.9 %copy-start.6 = (s32[1,16]{1,0:T(1,128)S(1)}, s32[1,16]{1,0:T(1,128)}, u32[]{:S(2)}) copy-start(s32[1,16]{1,0:T(1,128)} %perm_ref.1) | copy-start | bytes 196
  126.5 3.2 %copy-start = (bf16[32,16,32,192]{3,2,1,0:T(8,128)(2,1)}, bf16[32,16,32,192]{3,2,1,0:T(8,128)(2,1)S(1)}, u32[]{:S(2)}) copy-start(bf16[32,16,32,192]{3,2,1,0:T(8,128)(2,1)S(1)} %get-tuple-element.10.w_ref) | copy-start | bytes 18874372
  129.8 2.0 copy-start.1
  201.0 0.9 copy-start.2

commit v3 on v2

--- a/solution.py
+++ b/solution.py
@@ -172,32 +172,6 @@
     return copies
 
 
-def ring_gather(links, me, n, own_ref, all_ref):
-    rows = own_ref.shape[0] // 2
-    right, left = {"ctx": lax.rem(me + 1, n)}, {"ctx": lax.rem(me + n - 1, n)}
-    part = [pl.ds(0, rows), pl.ds(rows, rows)]
-    far = n // 2
-    ahead, back = {}, {}
-    for half in range(2):
-        ahead[1, half] = links.start(own_ref.at[part[half]], all_ref.at[me, part[half]], right)
-        back[1, half] = links.start(own_ref.at[part[half]], all_ref.at[me, part[half]], left)
-    for step in range(1, far):
-        below, above = lax.rem(me + n - step, n), lax.rem(me + step, n)
-        yield
-        for half in range(2):
-            ahead[step, half].wait_recv()
-            if step < far - 1 or half == 0:
-                ref = all_ref.at[below, part[half]]
-                ahead[step + 1, half] = links.start(ref, ref, right)
-            back[step, half].wait_recv()
-            if step < far - 1 or half == 1:
-                ref = all_ref.at[above, part[half]]
-                back[step + 1, half] = links.start(ref, ref, left)
-    yield
-    ahead[far, 0].wait_recv()
-    back[far, 1].wait_recv()
-
-
 def plane_gather(links, own_ref, all_ref, side=4):
     dp = lax.axis_index("dp")
     core = lax.rem(dp, 2)
@@ -296,66 +270,61 @@
     return barrier, len(axis_peers)
 
 
-def gather_kernel(n, packed_ref, tokens_ref, w_ref, recv_ref, tokens_all_ref, w_all_ref, w_rows, send_sem, recv_sem, local_sem):
+def ring_peers(me, n):
+    return [{"ctx": lax.rem(me + step, n)} for step in range(1, n)]
+
+
+def plane_peers(dp, planes):
+    return [{"dp": lax.rem(dp + step, planes)} for step in range(1, planes)]
+
+
+def gather_kernel(n, packed_ref, tokens_ref, w_ref, recv_ref, tokens_all_ref, w_rows_ref, send_sem, recv_sem, local_sem):
     me = lax.axis_index("ctx")
     dp = lax.axis_index("dp")
     core = lax.rem(dp, 2)
     chip = lax.div(dp, 2)
     x, y = lax.rem(chip, 4), lax.div(chip, 4)
-    peers = [{"ctx": lax.rem(me + step, n)} for step in range(1, n)]
+    peers = ring_peers(me, n)
     peers += [{"dp": dp + 1 - 2 * core}]
     peers += [{"dp": (y * 4 + lax.rem(x + step, 4)) * 2 + core} for step in (1, 3)]
     peers += [{"dp": (lax.rem(y + step, 4) * 4 + x) * 2 + core} for step in (1, 3)]
     barrier, count = greet(peers)
     links = Links(send_sem, recv_sem)
-    own_w = pltpu.make_async_copy(w_ref, w_rows.at[me], local_sem.at[0])
-    own_w.start()
-    own_block = pltpu.make_async_copy(packed_ref.at[me], recv_ref.at[me], local_sem.at[1])
-    own_block.start()
-    own_tokens = pltpu.make_async_copy(tokens_ref, tokens_all_ref.at[me], local_sem.at[2])
-    own_tokens.start()
+    own = [
+        pltpu.make_async_copy(packed_ref.at[me], recv_ref.at[me], local_sem.at[0]),
+        pltpu.make_async_copy(tokens_ref, tokens_all_ref.at[dp], local_sem.at[1]),
+        pltpu.make_async_copy(w_ref, w_rows_ref.at[me], local_sem.at[2]),
+    ]
+    for copy in own:
+        copy.start()
     pl.semaphore_wait(barrier, count)
-    rows_in = []
+    plane = plane_gather(links, tokens_ref, tokens_all_ref)
+    next(plane)
+    copies = all_to_all_start(links, "ctx", me, n, packed_ref, recv_ref)
     for step in far_first(n):
-        rows_in.append(links.start(w_ref, w_rows.at[me], {"ctx": lax.rem(me + step, n)}))
-    ring = ring_gather(links, me, n, tokens_ref, tokens_all_ref)
-    next(ring)
-    blocks_in = all_to_all_start(links, "ctx", me, n, packed_ref, recv_ref)
-    own_w.wait()
-    for copy in rows_in:
-        copy.wait_recv()
-    own_rows = pltpu.make_async_copy(w_rows, w_all_ref.at[dp], local_sem.at[0])
-    own_rows.start()
-    plane = plane_gather(links, w_rows, w_all_ref)
-    going = [plane, ring]
-    while going:
-        for chain in list(going):
-            try:
-                next(chain)
-            except StopIteration:
-                going.remove(chain)
-    for copy in blocks_in:
+        copies.append(links.start(w_ref, w_rows_ref.at[me], {"ctx": lax.rem(me + step, n)}))
+    for _ in plane:
+        pass
+    for copy in copies:
         copy.wait_recv()
     links.wait_sends()
-    own_rows.wait()
-    own_block.wait()
-    own_tokens.wait()
+    for copy in own:
+        copy.wait()
 
 
 def gather(packed, tokens, w, planes):
     n = packed.shape[0]
-    copies = (n - 1) * 2 + 2 * (n - 1) + PLANE_COPIES
+    copies = (n - 1) * 2 + PLANE_COPIES
     return pl.pallas_call(
         functools.partial(gather_kernel, n),
         out_shape=(
             jax.ShapeDtypeStruct(packed.shape, packed.dtype),
-            jax.ShapeDtypeStruct((n,) + tokens.shape, tokens.dtype),
-            jax.ShapeDtypeStruct((planes, n) + w.shape, w.dtype),
+            jax.ShapeDtypeStruct((planes,) + tokens.shape, tokens.dtype),
+            jax.ShapeDtypeStruct((n,) + w.shape, w.dtype),
         ),
         in_specs=[VMEM, VMEM, VMEM],
-        out_specs=(VMEM, ANY, ANY),
+        out_specs=(VMEM, ANY, VMEM),
         scratch_shapes=[
-            pltpu.VMEM((n,) + w.shape, w.dtype),
             pltpu.SemaphoreType.DMA((copies,)),
             pltpu.SemaphoreType.DMA((copies,)),
             pltpu.SemaphoreType.DMA((3,)),
@@ -366,54 +335,159 @@
     )(packed, tokens, w)
 
 
-def return_kernel(n, planes, grad_ref, part_ref, back_ref, parts_ref, send_sem, recv_sem, local_sem):
+def return_kernel(n, planes, grad_ref, w_rows_ref, back_ref, cols_ref, w_all_ref, send_sem, recv_sem, local_sem):
     me = lax.axis_index("ctx")
     dp = lax.axis_index("dp")
-    peers = [{"ctx": lax.rem(me + step, n)} for step in range(1, n)]
-    peers += [{"dp": lax.rem(dp + step, planes)} for step in range(1, planes)]
-    barrier, count = greet(peers)
+    half = cols_ref.shape[1]
+    barrier, count = greet(ring_peers(me, n) + plane_peers(dp, planes))
     own_block = pltpu.make_async_copy(grad_ref.at[me], back_ref.at[me], local_sem.at[0])
     own_block.start()
-    own_part = pltpu.make_async_copy(part_ref.at[dp], parts_ref.at[dp], local_sem.at[1])
-    own_part.start()
+    own_rows = pltpu.make_async_copy(w_rows_ref, w_all_ref.at[dp], local_sem.at[1])
+    own_rows.start()
     pl.semaphore_wait(barrier, count)
     links = Links(send_sem, recv_sem)
     copies = all_to_all_start(links, "ctx", me, n, grad_ref, back_ref)
-    copies += all_to_all_start(links, "dp", dp, planes, part_ref, parts_ref)
+    for _ in plane_gather(links, w_rows_ref, w_all_ref):
+        pass
     own_block.wait()
-    own_part.wait()
     for copy in copies:
-        copy.wait()
-
-
-def send_back(grad_t, parts):
-    n, planes = grad_t.shape[0], parts.shape[0]
-    copies = n + planes - 2
+        copy.wait_recv()
+
+    def chunk(owner):
+        start = pl.multiple_of(lax.rem(owner, 2) * half, half)
+        return back_ref.at[lax.div(owner, 2), pl.ds(start, half)]
+
+    copies = []
+    for step in far_first(planes):
+        owner = lax.rem(dp + step, planes)
+        copies.append(links.start(chunk(owner), cols_ref.at[dp], {"dp": owner}))
+    own_cols = pltpu.make_async_copy(chunk(dp), cols_ref.at[dp], local_sem.at[2])
+    own_cols.start()
+    for copy in copies:
+        copy.wait_recv()
+    links.wait_sends()
+    own_rows.wait()
+    own_cols.wait()
+
+
+def send_back(grad_t, w_rows, planes):
+    n, columns, tokens = grad_t.shape
+    copies = n - 1 + planes - 1 + PLANE_COPIES
     return pl.pallas_call(
         functools.partial(return_kernel, n, planes),
         out_shape=(
             jax.ShapeDtypeStruct(grad_t.shape, grad_t.dtype),
-            jax.ShapeDtypeStruct(parts.shape, parts.dtype),
+            jax.ShapeDtypeStruct((planes, n * columns // planes, tokens), grad_t.dtype),
+            jax.ShapeDtypeStruct((planes,) + w_rows.shape, w_rows.dtype),
         ),
         in_specs=[VMEM, VMEM],
-        out_specs=(VMEM, VMEM),
+        out_specs=(VMEM, VMEM, ANY),
         scratch_shapes=[
             pltpu.SemaphoreType.DMA((copies,)),
             pltpu.SemaphoreType.DMA((copies,)),
-            pltpu.SemaphoreType.DMA((2,)),
+            pltpu.SemaphoreType.DMA((3,)),
         ],
         compiler_params=pltpu.CompilerParams(
             collective_id=2, has_side_effects=True, vmem_limit_bytes=16 << 20
         ),
-    )(grad_t, parts)
+    )(grad_t, w_rows)
+
+
+def weight_grad_kernel(cols_ref, tokens_ref, out_ref, total):
+    step = pl.program_id(0)
+    group, tokens, width = tokens_ref.shape
+    left = jnp.concatenate([cols_ref[i] for i in range(group)], axis=1)
+    term = jnp.dot(left, tokens_ref[...].reshape(group * tokens, width), preferred_element_type=jnp.float32)
+
+    @pl.when(step == 0)
+    def _():
+        total[...] = term
+
+    @pl.when(step > 0)
+    def _():
+        total[...] += term
+
+    @pl.when(step == pl.num_programs(0) - 1)
+    def _():
+        planes, rows, columns = out_ref.shape
+        mean = total[...] * (1.0 / planes)
+        out_ref[...] = mean.T.astype(out_ref.dtype).reshape(planes, rows, columns)
+
+
+def weight_grad(cols, tokens_all):
+    planes, columns, tokens = cols.shape
+    width = tokens_all.shape[2]
+    group = 4
+    return pl.pallas_call(
+        weight_grad_kernel,
+        grid=(planes // group,),
+        out_shape=jax.ShapeDtypeStruct((planes, width // planes, columns), jnp.bfloat16),
+        in_specs=[
+            pl.BlockSpec((group, columns, tokens), lambda i: (i, 0, 0)),
+            pl.BlockSpec((group, tokens, width), lambda i: (i, 0, 0)),
+        ],
+        out_specs=pl.BlockSpec((planes, width // planes, columns), lambda i: (0, 0, 0)),
+        scratch_shapes=[pltpu.VMEM((columns, width), jnp.float32)],
+        compiler_params=pltpu.CompilerParams(dimension_semantics=("arbitrary",)),
+    )(cols, tokens_all)
+
+
+def settle_kernel(n, planes, part_ref, out_ref, rows_ref, send_sem, recv_sem, local_sem):
+    me = lax.axis_index("ctx")
+    dp = lax.axis_index("dp")
+    pair = planes // n
+    barrier, count = greet(ring_peers(me, n) + plane_peers(dp, planes))
+    own_part = pltpu.make_async_copy(part_ref.at[dp], rows_ref.at[dp], local_sem.at[0])
+    own_part.start()
+    pl.semaphore_wait(barrier, count)
+    links = Links(send_sem, recv_sem)
+    for copy in all_to_all_start(links, "dp", dp, planes, part_ref, rows_ref):
+        copy.wait_recv()
+    own_part.wait()
+
+    def head(owner):
+        return rows_ref.at[pl.ds(owner * pair, pair)]
+
+    copies = []
+    for step in far_first(n):
+        owner = lax.rem(me + step, n)
+        copies.append(links.start(head(owner), out_ref.at[me], {"ctx": owner}))
+    own_head = pltpu.make_async_copy(head(me), out_ref.at[me], local_sem.at[1])
+    own_head.start()
+    for copy in copies:
+        copy.wait_recv()
+    links.wait_sends()
+    own_head.wait()
+
+
+def settle(parts, n):
+    planes, rows, columns = parts.shape
+    copies = n - 1 + planes - 1
+    return pl.pallas_call(
+        functools.partial(settle_kernel, n, planes),
+        out_shape=jax.ShapeDtypeStruct((n, planes // n, rows, columns), parts.dtype),
+        in_specs=[VMEM],
+        out_specs=VMEM,
+        scratch_shapes=[
+            pltpu.VMEM(parts.shape, parts.dtype),
+            pltpu.SemaphoreType.DMA((copies,)),
+            pltpu.SemaphoreType.DMA((copies,)),
+            pltpu.SemaphoreType.DMA((2,)),
+        ],
+        compiler_params=pltpu.CompilerParams(
+            collective_id=3, has_side_effects=True, vmem_limit_bytes=16 << 20
+        ),
+    )(parts)
 
 
 def input_grad_kernel(back_ref, w_ref, out_ref, total):
     step = pl.program_id(0)
     planes, group, rows, columns = w_ref.shape
-    block = w_ref[:, 0].reshape(planes * rows, columns)
-    term = jnp.dot(block, back_ref[0], preferred_element_type=jnp.float32)
-    term = term.astype(jnp.bfloat16).astype(jnp.float32)
+    term = jnp.zeros(total.shape, jnp.float32)
+    for i in range(group):
+        block = w_ref[:, i].reshape(planes * rows, columns)
+        part = jnp.dot(block, back_ref[i], preferred_element_type=jnp.float32)
+        term = term + part.astype(jnp.bfloat16).astype(jnp.float32)
 
     @pl.when(step == 0)
     def _():
@@ -432,13 +506,14 @@
     n, columns, tokens = back_t.shape
     planes, _, rows, _ = w_all.shape
     width = planes * rows
+    group = 4
     return pl.pallas_call(
         input_grad_kernel,
-        grid=(n,),
+        grid=(n // group,),
         out_shape=jax.ShapeDtypeStruct((tokens, width), jnp.bfloat16),
         in_specs=[
-            pl.BlockSpec((1, columns, tokens), lambda i: (i, 0, 0)),
-            pl.BlockSpec((planes, 1, rows, columns), lambda i: (0, i, 0, 0)),
+            pl.BlockSpec((group, columns, tokens), lambda i: (i, 0, 0)),
+            pl.BlockSpec((planes, group, rows, columns), lambda i: (0, i, 0, 0)),
         ],
         out_specs=pl.BlockSpec((tokens, width), lambda i: (0, 0)),
         scratch_shapes=[pltpu.VMEM((width, tokens), jnp.float32)],
@@ -459,17 +534,12 @@
         ],
         axis=2,
     ).transpose(1, 0, 2)
-    blocks, tokens_all, w_all = gather(packed, layer_input[0], w_qkv, data_count)
+    blocks, tokens_all, w_rows = gather(packed, layer_input[0], w_qkv, data_count)
     grad_t = attention(blocks, lengths, block_perm)
-    weight_local = lax.dot_general(
-        tokens_all.reshape(ctx_count * tokens_dev, width),
-        grad_t.transpose(1, 0, 2).reshape(columns, ctx_count * tokens_dev),
-        (((0,), (1,)), ((), ())),
-        preferred_element_type=jnp.float32,
-    )
-    parts = weight_local.reshape(data_count, width // data_count, columns)
-    back_t, parts = send_back(grad_t, parts)
-    grad_weight = jnp.sum(parts, axis=0) * (1.0 / data_count)
+    back_t, cols, w_all = send_back(grad_t, w_rows, data_count)
+    parts = settle(weight_grad(cols, tokens_all), ctx_count)
+    grad_weight = jnp.sum(parts.astype(jnp.float32), axis=0).transpose(1, 0, 2)
+    grad_weight = grad_weight.reshape(width // data_count, columns)
     return (input_grad(back_t, w_all)[None], grad_weight)
 
 

time: 216 us -> 203 us (0.940)
  Pallas kernels: 193 us -> 188 us
  local copies, waits for them, and re-layouts: 16.9 us -> 13.4 us
  matrix products: 3.46 us -> 0 us
    pallas_call x1, Pallas kernels: 122 us -> 74.1 us  [gather(): pl.pallas_call(functools.partial(gather_kernel, n), out_shape=(jax.ShapeD...]
    pallas_call x1 -> x3, Pallas kernels: 12.8 us -> 41.2 us  [the longest x1 26.6 us: settle(): pl.pallas_call(functools.partial(settle_kernel, n, planes), out_shape=jax...]
    pallas_call x1, Pallas kernels: 42.9 us -> 57.1 us  [send_back(): pl.pallas_call(functools.partial(return_kernel, n, planes), out_shape=(ja...]
    dot_general x1 -> x0, local copies, waits for them, and re-layouts: 6.47 us -> none  [body(): lax.dot_general(tokens_all.reshape(ctx_count * tokens_dev, width), grad_t...]
    dot_general x1 -> x0, matrix products: 3.46 us -> none  [body(): lax.dot_general(tokens_all.reshape(ctx_count * tokens_dev, width), grad_t...]
    unnamed x16 -> x20, local copies, waits for them, and re-layouts: 8.81 us -> 11.9 us
where the time goes in v3:
time: 203 us; the launch traced here: 202 us
  Pallas kernels  188 us (93%)
  local copies, waits for them, and re-layouts  13.4 us (7%)
    pallas_call x1, Pallas kernels, gather(): pl.pallas_call(functools.partial(gather_kernel, n), out_shape=(jax.ShapeD...  74.1 us
    pallas_call x1, Pallas kernels, send_back(): pl.pallas_call(functools.partial(return_kernel, n, planes), out_shape=(ja...  57.1 us
    pallas_call x1, Pallas kernels, settle(): pl.pallas_call(functools.partial(settle_kernel, n, planes), out_shape=jax...  26.6 us
    pallas_call x1, Pallas kernels, attention(): pl.pallas_call(functools.partial(attention_kernel, tile), out_shape=jax.S...  15.5 us
    unnamed x20, local copies, waits for them, and re-layouts  11.9 us
    pallas_call x1, Pallas kernels, weight_grad(): pl.pallas_call(weight_grad_kernel, grid=(planes // group,), out_shape=jax...  7.89 us
    pallas_call x1, Pallas kernels, input_grad(): pl.pallas_call(input_grad_kernel, grid=(n // group,), out_shape=jax.Shape...  6.67 us

profile of v3, /device:TPU:1, one launch (start us, length us, event | category | flops | bytes accessed | tf_op | source)
XLA Modules:
  0.0 202.5 jit_solution(13363675675916882089)
XLA Ops:
  0.6 1.1 copy.17
  1.8 0.3 copy.19
  2.0 1.5 copy.16
  3.6 0.0 copy-start.5
  3.6 0.0 copy-start.6
  3.6 0.5 copy.18
  4.1 0.0 copy-start.7
  4.1 0.0 copy-start.8
  4.1 0.3 maximum_bitcast_fusion.packed_ref
  4.5 0.0 copy-done.5
  4.5 0.0 copy-done.6
  4.5 74.1 %shard_map.77 = (bf16[16,128,256]{2,1,0:T(8,128)(2,1)S(1)}, bf16[32,128,1024]{2,1,0:T(8,128)(2,1)S(1)}, bf16[16,32,192]{2,1,0:T(8,128)(2,1)S(1)}) custom-call(bf16[16,128,256]{2,1,0:T(8,128)(2,1)S(1)} %maximum_bitcast_fusion.packed_ref, bf16[128,1024]{1,0:T(8,128)(2,1)S(1)} %bitcast.7, bf16[32,192]{1,0:T(8,128)(2,1)S(1)} %copy-done.6), custom_call_target="tpu_custom_call" | custom-call | tf_op jit(solution)/shard_map/pallas_call | solution.py:318
  78.6 0.0 copy-start.1
  78.6 3.2 %copy-done.1 = bf16[32,128,1024]{2,1,0:T(8,128)(2,1)} copy-done((bf16[32,128,1024]{2,1,0:T(8,128)(2,1)}, bf16[32,128,1024]{2,1,0:T(8,128)(2,1)S(1)}, u32[]{:S(2)}) %copy-start.1) | copy-done | bytes 8388632
  81.8 0.0 copy-done.7
  81.8 0.0 copy-done.8
  81.8 15.5 %shard_map.78.grad_ref = bf16[16,192,128]{2,1,0:T(8,128)(2,1)S(1)} custom-call(s32[1,8]{1,0:T(1,128)S(1)} %copy-done.7, s32[1,16]{1,0:T(1,128)S(1)} %copy-done.8, bf16[16,128,256]{2,1,0:T(8,128)(2,1)S(1)} %get-tuple-element.8.x_ref), custom_call_target="tpu_custom_call" | custom-call | tf_op jit(solution)/shard_map/pallas_call | solution.py:115
  97.3 57.1 %shard_map.79 = (bf16[16,192,128]{2,1,0:T(8,128)(2,1)S(1)}, bf16[32,96,128]{2,1,0:T(8,128)(2,1)S(1)}, bf16[32,16,32,192]{3,2,1,0:T(8,128)(2,1)S(1)}) custom-call(bf16[16,192,128]{2,1,0:T(8,128)(2,1)S(1)} %shard_map.78.grad_ref, bf16[16,32,192]{2,1,0:T(8,128)(2,1)S(1)} %get-tuple-element.9.w_rows_ref), custom_call_target="tpu_custom_call" | custom-call | tf_op jit(solution)/shard_map/pallas_call | solution.py:376
  154.5 0.0 copy-start
  154.5 3.2 %copy-done = bf16[32,16,32,192]{3,2,1,0:T(8,128)(2,1)} copy-done((bf16[32,16,32,192]{3,2,1,0:T(8,128)(2,1)}, bf16[32,16,32,192]{3,2,1,0:T(8,128)(2,1)S(1)}, u32[]{:S(2)}) %copy-start) | copy-done | bytes 6291480
  157.7 0.0 copy-start.3
  157.7 0.9 copy-done.3
  158.6 0.0 copy-start.4
  158.6 0.9 copy-done.4
  159.5 7.9 %shard_map.81.part_ref = bf16[32,32,96]{2,1,0:T(8,128)(2,1)} custom-call(bf16[32,96,128]{2,1,0:T(8,128)(2,1)} %copy-done.4, bf16[32,128,1024]{2,1,0:T(8,128)(2,1)} %copy-done.1), custom_call_target="tpu_custom_call" | custom-call | tf_op jit(solution)/shard_map/pallas_call | solution.py:421
  167.4 0.0 copy-start.2
  167.4 0.9 copy-done.2
  168.3 26.6 %shard_map.82 = bf16[16,2,32,96]{3,2,1,0:T(8,128)(2,1)S(1)} custom-call(bf16[32,32,96]{2,1,0:T(8,128)(2,1)S(1)} %copy-done.2), custom_call_target="tpu_custom_call" | custom-call | tf_op jit(solution)/shard_map/pallas_call | solution.py:466
  195.0 0.1 convert_reduce_fusion
  195.1 0.7 reshape.7
  195.8 6.7 %shard_map.80 = bf16[128,1024]{1,0:T(8,128)(2,1)} custom-call(bf16[16,192,128]{2,1,0:T(8,128)(2,1)} %copy-done.3, bf16[32,16,32,192]{3,2,1,0:T(8,128)(2,1)} %copy-done), custom_call_target="tpu_custom_call" | custom-call | tf_op jit(solution)/shard_map/pallas_call | solution.py:510
  (1 shorter events, 0.0 us)
Async XLA Ops:
  3.6 1.0 copy-start.5
  3.6 0.9 copy-start.6
  4.1 77.7 %copy-start.7 = (s32[1,8]{1,0:T(1,128)S(1)}, s32[1,8]{1,0:T(1,128)}, u32[]{:S(2)}) copy-start(s32[1,8]{1,0:T(1,128)} %lengths_ref.1) | copy-start | bytes 100
  4.1 77.7 %copy-start.8 = (s32[1,16]{1,0:T(1,128)S(1)}, s32[1,16]{1,0:T(1,128)}, u32[]{:S(2)}) copy-start(s32[1,16]{1,0:T(1,128)} %perm_ref.1) | copy-start | bytes 196
  78.6 3.2 %copy-start.1 = (bf16[32,128,1024]{2,1,0:T(8,128)(2,1)}, bf16[32,128,1024]{2,1,0:T(8,128)(2,1)S(1)}, u32[]{:S(2)}) copy-start(bf16[32,128,1024]{2,1,0:T(8,128)(2,1)S(1)} %get-tuple-element.13.tokens_ref) | copy-start | bytes 25165828
  154.5 3.2 %copy-start = (bf16[32,16,32,192]{3,2,1,0:T(8,128)(2,1)}, bf16[32,16,32,192]{3,2,1,0:T(8,128)(2,1)S(1)}, u32[]{:S(2)}) copy-start(bf16[32,16,32,192]{3,2,1,0:T(8,128)(2,1)S(1)} %get-tuple-element.11.w_ref) | copy-start | bytes 18874372
  157.7 0.9 copy-start.3
  158.6 0.9 copy-start.4
  167.4 0.9 copy-start.2

commit v4 on v3

--- a/solution.py
+++ b/solution.py
@@ -11,7 +11,6 @@
 BLK = 128
 MESH = pl.DeviceIdType.MESH
 VMEM = pl.BlockSpec(memory_space=pltpu.VMEM)
-ANY = pl.BlockSpec(memory_space=pl.ANY)
 
 
 def attention_kernel(tile, lengths_ref, perm_ref, x_ref, out_ref, q_s, k_s, v_s, g_s, kt_s, gq_s, gk_s, gv_s, start_s, scale_s):
@@ -129,7 +128,7 @@
             pltpu.VMEM((whole // tile, tile), jnp.int32),
             pltpu.VMEM((whole // tile, tile), f32),
         ],
-        compiler_params=pltpu.CompilerParams(vmem_limit_bytes=32 << 20),
+        compiler_params=pltpu.CompilerParams(vmem_limit_bytes=24 << 20),
     )(lengths, perm, packed)
 
 
@@ -323,202 +322,131 @@
             jax.ShapeDtypeStruct((n,) + w.shape, w.dtype),
         ),
         in_specs=[VMEM, VMEM, VMEM],
-        out_specs=(VMEM, ANY, VMEM),
+        out_specs=(VMEM, VMEM, VMEM),
         scratch_shapes=[
             pltpu.SemaphoreType.DMA((copies,)),
             pltpu.SemaphoreType.DMA((copies,)),
             pltpu.SemaphoreType.DMA((3,)),
         ],
         compiler_params=pltpu.CompilerParams(
-            collective_id=1, has_side_effects=True, vmem_limit_bytes=16 << 20
+            collective_id=1, has_side_effects=True, vmem_limit_bytes=24 << 20
         ),
     )(packed, tokens, w)
 
 
-def return_kernel(n, planes, grad_ref, w_rows_ref, back_ref, cols_ref, w_all_ref, send_sem, recv_sem, local_sem):
+def return_kernel(
+    n, planes, grad_ref, w_rows_ref, tokens_ref, input_ref, weight_ref,
+    back, cols, w_all, input_sum, weight_sum, parts, rows_in, send_sem, recv_sem, local_sem,
+):
     me = lax.axis_index("ctx")
     dp = lax.axis_index("dp")
-    half = cols_ref.shape[1]
+    half = cols.shape[1]
+    pair = planes // n
     barrier, count = greet(ring_peers(me, n) + plane_peers(dp, planes))
-    own_block = pltpu.make_async_copy(grad_ref.at[me], back_ref.at[me], local_sem.at[0])
+    own_block = pltpu.make_async_copy(grad_ref.at[me], back.at[me], local_sem.at[0])
     own_block.start()
-    own_rows = pltpu.make_async_copy(w_rows_ref, w_all_ref.at[dp], local_sem.at[1])
+    own_rows = pltpu.make_async_copy(w_rows_ref, w_all.at[dp], local_sem.at[1])
     own_rows.start()
+    input_sum[...] = jnp.zeros_like(input_sum)
+    weight_sum[...] = jnp.zeros_like(weight_sum)
     pl.semaphore_wait(barrier, count)
     links = Links(send_sem, recv_sem)
-    copies = all_to_all_start(links, "ctx", me, n, grad_ref, back_ref)
-    for _ in plane_gather(links, w_rows_ref, w_all_ref):
+    copies = all_to_all_start(links, "ctx", me, n, grad_ref, back)
+    for _ in plane_gather(links, w_rows_ref, w_all):
         pass
     own_block.wait()
+    own_rows.wait()
     for copy in copies:
         copy.wait_recv()
 
     def chunk(owner):
         start = pl.multiple_of(lax.rem(owner, 2) * half, half)
-        return back_ref.at[lax.div(owner, 2), pl.ds(start, half)]
-
-    copies = []
+        return back.at[lax.div(owner, 2), pl.ds(start, half)]
+
+    own_cols = pltpu.make_async_copy(chunk(dp), cols.at[dp], local_sem.at[2])
+    own_cols.start()
+    arrivals = [(dp, own_cols)]
     for step in far_first(planes):
         owner = lax.rem(dp + step, planes)
-        copies.append(links.start(chunk(owner), cols_ref.at[dp], {"dp": owner}))
-    own_cols = pltpu.make_async_copy(chunk(dp), cols_ref.at[dp], local_sem.at[2])
-    own_cols.start()
+        source = lax.rem(dp + planes - step, planes)
+        arrivals.append((source, links.start(chunk(owner), cols.at[dp], {"dp": owner})))
+
+    def add_head(head, carry):
+        block = w_all[:, pl.ds(head, 1)].reshape(input_sum.shape[0], w_all.shape[3])
+        term = jnp.dot(block, back[head], preferred_element_type=jnp.float32)
+        input_sum[...] += term.astype(jnp.bfloat16).astype(jnp.float32)
+        return carry
+
+    group = 4
+    for first in range(0, planes, group):
+        members = arrivals[first : first + group]
+        for source, copy in members:
+            if copy is own_cols:
+                copy.wait()
+            else:
+                copy.wait_recv()
+        left = jnp.concatenate([cols[source] for source, _ in members], axis=1)
+        right = jnp.concatenate([tokens_ref[source] for source, _ in members], axis=0)
+        weight_sum[...] += jnp.dot(left, right, preferred_element_type=jnp.float32)
+
+    mean = weight_sum[...] * (1.0 / planes)
+    parts[...] = mean.T.astype(parts.dtype).reshape(parts.shape)
+    add_head(0, 0)
+    own_part = pltpu.make_async_copy(parts.at[dp], rows_in.at[dp], local_sem.at[0])
+    own_part.start()
+    copies = all_to_all_start(links, "dp", dp, planes, parts, rows_in)
+    lax.fori_loop(1, 8, add_head, 0)
+    own_part.wait()
+    for copy in copies:
+        copy.wait_recv()
+
+    def head_rows(owner):
+        return rows_in.at[pl.ds(owner * pair, pair)]
+
+    own_head = pltpu.make_async_copy(head_rows(me), weight_ref.at[me], local_sem.at[1])
+    own_head.start()
+    copies = []
+    for step in far_first(n):
+        owner = lax.rem(me + step, n)
+        copies.append(links.start(head_rows(owner), weight_ref.at[me], {"ctx": owner}))
+    lax.fori_loop(8, n, add_head, 0)
+    input_ref[...] = input_sum[...].T.astype(input_ref.dtype)
+    own_head.wait()
     for copy in copies:
         copy.wait_recv()
     links.wait_sends()
-    own_rows.wait()
-    own_cols.wait()
-
-
-def send_back(grad_t, w_rows, planes):
+
+
+def send_back(grad_t, w_rows, tokens_all):
     n, columns, tokens = grad_t.shape
-    copies = n - 1 + planes - 1 + PLANE_COPIES
+    planes, _, width = tokens_all.shape
+    rows, half = width // planes, n * columns // planes
+    copies = 2 * (n - 1) + 2 * (planes - 1) + PLANE_COPIES
+    bf, f32 = jnp.bfloat16, jnp.float32
     return pl.pallas_call(
         functools.partial(return_kernel, n, planes),
         out_shape=(
-            jax.ShapeDtypeStruct(grad_t.shape, grad_t.dtype),
-            jax.ShapeDtypeStruct((planes, n * columns // planes, tokens), grad_t.dtype),
-            jax.ShapeDtypeStruct((planes,) + w_rows.shape, w_rows.dtype),
+            jax.ShapeDtypeStruct((tokens, width), bf),
+            jax.ShapeDtypeStruct((n, planes // n, rows, half), bf),
         ),
-        in_specs=[VMEM, VMEM],
-        out_specs=(VMEM, VMEM, ANY),
+        in_specs=[VMEM, VMEM, VMEM],
+        out_specs=(VMEM, VMEM),
         scratch_shapes=[
+            pltpu.VMEM(grad_t.shape, bf),
+            pltpu.VMEM((planes, half, tokens), bf),
+            pltpu.VMEM((planes,) + w_rows.shape, bf),
+            pltpu.VMEM((width, tokens), f32),
+            pltpu.VMEM((half, width), f32),
+            pltpu.VMEM((planes, rows, half), bf),
+            pltpu.VMEM((planes, rows, half), bf),
             pltpu.SemaphoreType.DMA((copies,)),
             pltpu.SemaphoreType.DMA((copies,)),
             pltpu.SemaphoreType.DMA((3,)),
         ],
         compiler_params=pltpu.CompilerParams(
-            collective_id=2, has_side_effects=True, vmem_limit_bytes=16 << 20
+            collective_id=2, has_side_effects=True, vmem_limit_bytes=36 << 20
         ),
-    )(grad_t, w_rows)
-
-
-def weight_grad_kernel(cols_ref, tokens_ref, out_ref, total):
-    step = pl.program_id(0)
-    group, tokens, width = tokens_ref.shape
-    left = jnp.concatenate([cols_ref[i] for i in range(group)], axis=1)
-    term = jnp.dot(left, tokens_ref[...].reshape(group * tokens, width), preferred_element_type=jnp.float32)
-
-    @pl.when(step == 0)
-    def _():
-        total[...] = term
-
-    @pl.when(step > 0)
-    def _():
-        total[...] += term
-
-    @pl.when(step == pl.num_programs(0) - 1)
-    def _():
-        planes, rows, columns = out_ref.shape
-        mean = total[...] * (1.0 / planes)
-        out_ref[...] = mean.T.astype(out_ref.dtype).reshape(planes, rows, columns)
-
-
-def weight_grad(cols, tokens_all):
-    planes, columns, tokens = cols.shape
-    width = tokens_all.shape[2]
-    group = 4
-    return pl.pallas_call(
-        weight_grad_kernel,
-        grid=(planes // group,),
-        out_shape=jax.ShapeDtypeStruct((planes, width // planes, columns), jnp.bfloat16),
-        in_specs=[
-            pl.BlockSpec((group, columns, tokens), lambda i: (i, 0, 0)),
-            pl.BlockSpec((group, tokens, width), lambda i: (i, 0, 0)),
-        ],
-        out_specs=pl.BlockSpec((planes, width // planes, columns), lambda i: (0, 0, 0)),
-        scratch_shapes=[pltpu.VMEM((columns, width), jnp.float32)],
-        compiler_params=pltpu.CompilerParams(dimension_semantics=("arbitrary",)),
-    )(cols, tokens_all)
-
-
-def settle_kernel(n, planes, part_ref, out_ref, rows_ref, send_sem, recv_sem, local_sem):
-    me = lax.axis_index("ctx")
-    dp = lax.axis_index("dp")
-    pair = planes // n
-    barrier, count = greet(ring_peers(me, n) + plane_peers(dp, planes))
-    own_part = pltpu.make_async_copy(part_ref.at[dp], rows_ref.at[dp], local_sem.at[0])
-    own_part.start()
-    pl.semaphore_wait(barrier, count)
-    links = Links(send_sem, recv_sem)
-    for copy in all_to_all_start(links, "dp", dp, planes, part_ref, rows_ref):
-        copy.wait_recv()
-    own_part.wait()
-
-    def head(owner):
-        return rows_ref.at[pl.ds(owner * pair, pair)]
-
-    copies = []
-    for step in far_first(n):
-        owner = lax.rem(me + step, n)
-        copies.append(links.start(head(owner), out_ref.at[me], {"ctx": owner}))
-    own_head = pltpu.make_async_copy(head(me), out_ref.at[me], local_sem.at[1])
-    own_head.start()
-    for copy in copies:
-        copy.wait_recv()
-    links.wait_sends()
-    own_head.wait()
-
-
-def settle(parts, n):
-    planes, rows, columns = parts.shape
-    copies = n - 1 + planes - 1
-    return pl.pallas_call(
-        functools.partial(settle_kernel, n, planes),
-        out_shape=jax.ShapeDtypeStruct((n, planes // n, rows, columns), parts.dtype),
-        in_specs=[VMEM],
-        out_specs=VMEM,
-        scratch_shapes=[
-            pltpu.VMEM(parts.shape, parts.dtype),
-            pltpu.SemaphoreType.DMA((copies,)),
-            pltpu.SemaphoreType.DMA((copies,)),
-            pltpu.SemaphoreType.DMA((2,)),
-        ],
-        compiler_params=pltpu.CompilerParams(
-            collective_id=3, has_side_effects=True, vmem_limit_bytes=16 << 20
-        ),
-    )(parts)
-
-
-def input_grad_kernel(back_ref, w_ref, out_ref, total):
-    step = pl.program_id(0)
-    planes, group, rows, columns = w_ref.shape
-    term = jnp.zeros(total.shape, jnp.float32)
-    for i in range(group):
-        block = w_ref[:, i].reshape(planes * rows, columns)
-        part = jnp.dot(block, back_ref[i], preferred_element_type=jnp.float32)
-        term = term + part.astype(jnp.bfloat16).astype(jnp.float32)
-
-    @pl.when(step == 0)
-    def _():
-        total[...] = term
-
-    @pl.when(step > 0)
-    def _():
-        total[...] += term
-
-    @pl.when(step == pl.num_programs(0) - 1)
-    def _():
-        out_ref[...] = total[...].T.astype(out_ref.dtype)
-
-
-def input_grad(back_t, w_all):
-    n, columns, tokens = back_t.shape
-    planes, _, rows, _ = w_all.shape
-    width = planes * rows
-    group = 4
-    return pl.pallas_call(
-        input_grad_kernel,
-        grid=(n // group,),
-        out_shape=jax.ShapeDtypeStruct((tokens, width), jnp.bfloat16),
-        in_specs=[
-            pl.BlockSpec((group, columns, tokens), lambda i: (i, 0, 0)),
-            pl.BlockSpec((planes, group, rows, columns), lambda i: (0, i, 0, 0)),
-        ],
-        out_specs=pl.BlockSpec((tokens, width), lambda i: (0, 0)),
-        scratch_shapes=[pltpu.VMEM((width, tokens), jnp.float32)],
-        compiler_params=pltpu.CompilerParams(dimension_semantics=("arbitrary",)),
-    )(back_t, w_all)
+    )(grad_t, w_rows, tokens_all)
 
 
 def body(layer_input, projected, grad_output, w_qkv, lengths, block_perm):
@@ -536,11 +464,10 @@
     ).transpose(1, 0, 2)
     blocks, tokens_all, w_rows = gather(packed, layer_input[0], w_qkv, data_count)
     grad_t = attention(blocks, lengths, block_perm)
-    back_t, cols, w_all = send_back(grad_t, w_rows, data_count)
-    parts = settle(weight_grad(cols, tokens_all), ctx_count)
+    grad_input, parts = send_back(grad_t, w_rows, tokens_all)
     grad_weight = jnp.sum(parts.astype(jnp.float32), axis=0).transpose(1, 0, 2)
     grad_weight = grad_weight.reshape(width // data_count, columns)
-    return (input_grad(back_t, w_all)[None], grad_weight)
+    return (grad_input[None], grad_weight)
 
 
 def solution(mesh):

time: 203 us -> 175 us (0.86)
  Pallas kernels: 188 us -> 169 us
  local copies, waits for them, and re-layouts: 13.4 us -> 4.93 us
    pallas_call x3 -> x0, Pallas kernels: 41.2 us -> none  [the longest x1 26.6 us: settle(): pl.pallas_call(functools.partial(settle_kernel, n, planes), out_shape=jax...]
    pallas_call x1, Pallas kernels: 57.1 us -> 80.8 us  [send_back(): pl.pallas_call(functools.partial(return_kernel, n, planes), out_shape=(ja...]
    unnamed x20 -> x11, local copies, waits for them, and re-layouts: 11.9 us -> 3.4 us
where the time goes in v4:
time: 175 us
  Pallas kernels  169 us (97%)
  local copies, waits for them, and re-layouts  4.93 us (3%)
    pallas_call x1, Pallas kernels, send_back(): pl.pallas_call(functools.partial(return_kernel, n, planes), out_shape=(ja...  80.8 us
    pallas_call x1, Pallas kernels, gather(): pl.pallas_call(functools.partial(gather_kernel, n), out_shape=(jax.ShapeD...  74.1 us
    pallas_call x1, Pallas kernels, attention(): pl.pallas_call(functools.partial(attention_kernel, tile), out_shape=jax.S...  13.8 us

profile of v4, /device:TPU:1, one launch (start us, length us, event | category | flops | bytes accessed | tf_op | source)
XLA Modules:
  0.0 174.7 jit_solution(15032496891308880574)
XLA Ops:
  0.6 1.1 copy.17
  1.8 0.3 copy.19
  2.0 1.5 copy.16
  3.6 0.0 copy-start
  3.6 0.0 copy-start.1
  3.6 0.5 copy.18
  4.1 0.0 copy-start.2
  4.1 0.0 copy-start.3
  4.1 0.3 maximum_bitcast_fusion.packed_ref
  4.5 0.0 copy-done
  4.5 0.0 copy-done.1
  4.5 74.1 %shard_map.77 = (bf16[16,128,256]{2,1,0:T(8,128)(2,1)S(1)}, bf16[32,128,1024]{2,1,0:T(8,128)(2,1)S(1)}, bf16[16,32,192]{2,1,0:T(8,128)(2,1)S(1)}) custom-call(bf16[16,128,256]{2,1,0:T(8,128)(2,1)S(1)} %maximum_bitcast_fusion.packed_ref, bf16[128,1024]{1,0:T(8,128)(2,1)S(1)} %bitcast.8, bf16[32,192]{1,0:T(8,128)(2,1)S(1)} %copy-done.1), custom_call_target="tpu_custom_call" | custom-call | tf_op jit(solution)/shard_map/pallas_call | solution.py:317
  78.6 0.0 copy-done.2
  78.6 0.0 copy-done.3
  78.6 13.8 %shard_map.78.grad_ref = bf16[16,192,128]{2,1,0:T(8,128)(2,1)S(1)} custom-call(s32[1,8]{1,0:T(1,128)S(1)} %copy-done.2, s32[1,16]{1,0:T(1,128)S(1)} %copy-done.3, bf16[16,128,256]{2,1,0:T(8,128)(2,1)S(1)} %get-tuple-element.7.x_ref), custom_call_target="tpu_custom_call" | custom-call | tf_op jit(solution)/shard_map/pallas_call | solution.py:114
  92.4 80.8 %shard_map.79 = (bf16[128,1024]{1,0:T(8,128)(2,1)S(1)}, bf16[16,2,32,96]{3,2,1,0:T(8,128)(2,1)S(1)}) custom-call(bf16[16,192,128]{2,1,0:T(8,128)(2,1)S(1)} %shard_map.78.grad_ref, bf16[16,32,192]{2,1,0:T(8,128)(2,1)S(1)} %get-tuple-element.8.w_rows_ref, bf16[32,128,1024]{2,1,0:T(8,128)(2,1)S(1)} %get-tuple-element.9.tokens_ref), custom_call_target="tpu_custom_call" | custom-call | tf_op jit(solution)/shard_map/pallas_call | solution.py:426
  173.2 0.1 convert_reduce_fusion
  173.3 0.7 reshape.7
  174.0 0.7 copy.22
  (1 shorter events, 0.0 us)
Async XLA Ops:
  3.6 1.0 copy-start
  3.6 0.9 copy-start.1
  4.1 74.5 %copy-start.2 = (s32[1,8]{1,0:T(1,128)S(1)}, s32[1,8]{1,0:T(1,128)}, u32[]{:S(2)}) copy-start(s32[1,8]{1,0:T(1,128)} %lengths_ref.1) | copy-start | bytes 100
  4.1 74.5 %copy-start.3 = (s32[1,16]{1,0:T(1,128)S(1)}, s32[1,16]{1,0:T(1,128)}, u32[]{:S(2)}) copy-start(s32[1,16]{1,0:T(1,128)} %perm_ref.1) | copy-start | bytes 196

commit v5 on v4

--- a/solution.py
+++ b/solution.py
@@ -9,8 +9,13 @@
 
 DH = 64
 BLK = 128
+LAG = 5
 MESH = pl.DeviceIdType.MESH
 VMEM = pl.BlockSpec(memory_space=pltpu.VMEM)
+
+
+def sigmoid(value):
+    return 0.5 * jnp.tanh(0.5 * value) + 0.5
 
 
 def attention_kernel(tile, lengths_ref, perm_ref, x_ref, out_ref, q_s, k_s, v_s, g_s, kt_s, gq_s, gk_s, gv_s, start_s, scale_s):
@@ -32,12 +37,12 @@
     start_s[...] = first
     scale_s[...] = lax.rsqrt(length.astype(jnp.float32))
 
-    @pl.loop(0, slots)
+    @pl.loop(0, slots, unroll=4)
     def _(slot):
         row = pl.multiple_of(perm_ref[0, slot] * BLK, BLK)
         block = x_ref[slot]
         pre = block[:, : 3 * DH].astype(jnp.float32)
-        active = (pre * jax.nn.sigmoid(pre)).astype(jnp.bfloat16)
+        active = (pre * sigmoid(pre)).astype(jnp.bfloat16)
         q_s[pl.ds(row, BLK), :] = active[:, :DH] * jnp.bfloat16(0.0625)
         key = active[:, DH : 2 * DH]
         k_s[pl.ds(row, BLK), :] = key
@@ -79,8 +84,9 @@
             up = 1.0 + th
             w = half * up
             slope = up + w * (1.0 - th)
-            weights = jnp.where(visible, w * scale_row, 0.0).astype(jnp.bfloat16)
-            gs = jnp.where(visible, gw * slope * scale_row, 0.0).astype(jnp.bfloat16)
+            scale = jnp.where(visible, scale_row, 0.0)
+            weights = (w * scale).astype(jnp.bfloat16)
+            gs = (gw * slope * scale).astype(jnp.bfloat16)
             gv = gv + jnp.dot(weights, grads, preferred_element_type=jnp.float32)
             gk = gk + jnp.dot(gs, queries, preferred_element_type=jnp.float32)
             gq_s[:, pl.ds(query_row, tile)] += jnp.dot(keys_t, gs, preferred_element_type=jnp.float32)
@@ -91,11 +97,11 @@
         gk_s[pl.ds(key_row, tile), :] = gk
         gv_s[pl.ds(key_row, tile), :] = gv
 
-    @pl.loop(0, slots)
+    @pl.loop(0, slots, unroll=4)
     def _(slot):
         row = pl.multiple_of(perm_ref[0, slot] * BLK, BLK)
         pre = x_ref[slot][:, : 3 * DH].astype(jnp.float32)
-        sigma = jax.nn.sigmoid(pre)
+        sigma = sigmoid(pre)
         slope = sigma * (1.0 + pre * (1.0 - sigma))
         gq = gq_s[:, pl.ds(row, BLK)].T * 0.0625
         gk = gk_s[pl.ds(row, BLK), :]
@@ -277,7 +283,9 @@
     return [{"dp": lax.rem(dp + step, planes)} for step in range(1, planes)]
 
 
-def gather_kernel(n, packed_ref, tokens_ref, w_ref, recv_ref, tokens_all_ref, w_rows_ref, send_sem, recv_sem, local_sem):
+def gather_kernel(
+    n, pre_ref, grad_ref, tokens_ref, w_ref, recv_ref, tokens_all_ref, w_rows_ref, packed_ref, send_sem, recv_sem, local_sem
+):
     me = lax.axis_index("ctx")
     dp = lax.axis_index("dp")
     core = lax.rem(dp, 2)
@@ -289,14 +297,19 @@
     peers += [{"dp": (lax.rem(y + step, 4) * 4 + x) * 2 + core} for step in (1, 3)]
     barrier, count = greet(peers)
     links = Links(send_sem, recv_sem)
+    columns = 3 * DH
+    for head in range(n):
+        packed_ref[head, :, :columns] = pre_ref[:, head * columns : (head + 1) * columns]
+        packed_ref[head, :, columns:] = grad_ref[:, head * DH : (head + 1) * DH]
     own = [
-        pltpu.make_async_copy(packed_ref.at[me], recv_ref.at[me], local_sem.at[0]),
         pltpu.make_async_copy(tokens_ref, tokens_all_ref.at[dp], local_sem.at[1]),
         pltpu.make_async_copy(w_ref, w_rows_ref.at[me], local_sem.at[2]),
     ]
     for copy in own:
         copy.start()
     pl.semaphore_wait(barrier, count)
+    own.append(pltpu.make_async_copy(packed_ref.at[me], recv_ref.at[me], local_sem.at[0]))
+    own[-1].start()
     plane = plane_gather(links, tokens_ref, tokens_all_ref)
     next(plane)
     copies = all_to_all_start(links, "ctx", me, n, packed_ref, recv_ref)
@@ -311,19 +324,20 @@
         copy.wait()
 
 
-def gather(packed, tokens, w, planes):
-    n = packed.shape[0]
+def gather(pre, grads, tokens, w, n, planes):
     copies = (n - 1) * 2 + PLANE_COPIES
+    packed = (n, tokens.shape[0], 4 * DH)
     return pl.pallas_call(
         functools.partial(gather_kernel, n),
         out_shape=(
-            jax.ShapeDtypeStruct(packed.shape, packed.dtype),
+            jax.ShapeDtypeStruct(packed, pre.dtype),
             jax.ShapeDtypeStruct((planes,) + tokens.shape, tokens.dtype),
             jax.ShapeDtypeStruct((n,) + w.shape, w.dtype),
         ),
-        in_specs=[VMEM, VMEM, VMEM],
+        in_specs=[VMEM, VMEM, VMEM, VMEM],
         out_specs=(VMEM, VMEM, VMEM),
         scratch_shapes=[
+            pltpu.VMEM(packed, pre.dtype),
             pltpu.SemaphoreType.DMA((copies,)),
             pltpu.SemaphoreType.DMA((copies,)),
             pltpu.SemaphoreType.DMA((3,)),
@@ -331,12 +345,12 @@
         compiler_params=pltpu.CompilerParams(
             collective_id=1, has_side_effects=True, vmem_limit_bytes=24 << 20
         ),
-    )(packed, tokens, w)
+    )(pre, grads, tokens, w)
 
 
 def return_kernel(
     n, planes, grad_ref, w_rows_ref, tokens_ref, input_ref, weight_ref,
-    back, cols, w_all, input_sum, weight_sum, parts, rows_in, send_sem, recv_sem, local_sem,
+    back, cols, w_all, input_sum, weight_sum, parts, rows_in, send_sem, recv_sem, forward_send, forward_recv, local_sem,
 ):
     me = lax.axis_index("ctx")
     dp = lax.axis_index("dp")
@@ -351,25 +365,40 @@
     weight_sum[...] = jnp.zeros_like(weight_sum)
     pl.semaphore_wait(barrier, count)
     links = Links(send_sem, recv_sem)
-    copies = all_to_all_start(links, "ctx", me, n, grad_ref, back)
-    for _ in plane_gather(links, w_rows_ref, w_all):
-        pass
-    own_block.wait()
-    own_rows.wait()
-    for copy in copies:
-        copy.wait_recv()
-
-    def chunk(owner):
-        start = pl.multiple_of(lax.rem(owner, 2) * half, half)
-        return back.at[lax.div(owner, 2), pl.ds(start, half)]
-
-    own_cols = pltpu.make_async_copy(chunk(dp), cols.at[dp], local_sem.at[2])
-    own_cols.start()
-    arrivals = [(dp, own_cols)]
-    for step in far_first(planes):
-        owner = lax.rem(dp + step, planes)
-        source = lax.rem(dp + planes - step, planes)
-        arrivals.append((source, links.start(chunk(owner), cols.at[dp], {"dp": owner})))
+    turn = lax.rem(lax.div(dp, 2), n - 1)
+    arrivals = []
+    for place in range(n - 1):
+        index = lax.rem(turn + place, n - 1)
+        odd, near = lax.rem(index, 2), lax.div(index, 2)
+        step = (near + 1) * (1 - odd) + (n - 1 - near) * odd
+        peer = lax.rem(me + step, n)
+        copy = links.start(grad_ref.at[peer], back.at[me], {"ctx": peer})
+        arrivals.append((lax.rem(me + n - step, n), copy))
+
+    def forward(head, place, source):
+        for side in range(2):
+            owner = head * 2 + side
+            chunk = source.at[head, pl.ds(side * half, half)]
+
+            def to_owner(chunk=chunk, owner=owner, side=side):
+                return pltpu.make_async_remote_copy(
+                    src_ref=chunk,
+                    dst_ref=cols.at[dp],
+                    send_sem=forward_send.at[2 * place + side],
+                    recv_sem=forward_recv.at[dp],
+                    device_id={"dp": owner},
+                    device_id_type=MESH,
+                )
+
+            @pl.when(owner != dp)
+            def _():
+                to_owner().start()
+
+            @pl.when(owner == dp)
+            def _():
+                pltpu.make_async_copy(chunk, cols.at[dp], forward_recv.at[dp]).start()
+
+            sent.append((owner, to_owner))
 
     def add_head(head, carry):
         block = w_all[:, pl.ds(head, 1)].reshape(input_sum.shape[0], w_all.shape[3])
@@ -377,17 +406,40 @@
         input_sum[...] += term.astype(jnp.bfloat16).astype(jnp.float32)
         return carry
 
-    group = 4
-    for first in range(0, planes, group):
-        members = arrivals[first : first + group]
-        for source, copy in members:
-            if copy is own_cols:
-                copy.wait()
-            else:
-                copy.wait_recv()
-        left = jnp.concatenate([cols[source] for source, _ in members], axis=1)
-        right = jnp.concatenate([tokens_ref[source] for source, _ in members], axis=0)
+    ahead = lax.rem(me + n - lax.div(dp, 2), n)
+    short = lax.div(n + n // 2 - ahead, n)
+    own_place = short * 2 * (ahead - 1) + (1 - short) * (2 * n - 1 - 2 * ahead)
+
+    def add_sources(first):
+        sources = []
+        for place in range(first, first + 2):
+            chip = n - 1 if place == n - 1 else lax.rem(own_place - place + 2 * n - 2, n - 1)
+            sources += [2 * chip, 2 * chip + 1]
+        for source in sources:
+            pltpu.make_async_copy(cols.at[source], cols.at[source], forward_recv.at[source]).wait()
+        left = jnp.concatenate([cols[source] for source in sources], axis=1)
+        right = jnp.concatenate([tokens_ref[source] for source in sources], axis=0)
         weight_sum[...] += jnp.dot(left, right, preferred_element_type=jnp.float32)
+
+    sent = []
+    forward(me, n - 1, grad_ref)
+    plane = plane_gather(links, w_rows_ref, w_all)
+    next(plane)
+    added = 0
+    for place, (head, copy) in enumerate(arrivals):
+        copy.wait_recv()
+        forward(head, place, back)
+        next(plane, None)
+        if place >= added + LAG and added + 1 < n:
+            add_sources(added)
+            added += 2
+    for _ in plane:
+        pass
+    own_block.wait()
+    own_rows.wait()
+    while added < n:
+        add_sources(added)
+        added += 2
 
     mean = weight_sum[...] * (1.0 / planes)
     parts[...] = mean.T.astype(parts.dtype).reshape(parts.shape)
@@ -415,13 +467,18 @@
     for copy in copies:
         copy.wait_recv()
     links.wait_sends()
+    for owner, to_owner in sent:
+
+        @pl.when(owner != dp)
+        def _():
+            to_owner().wait_send()
 
 
 def send_back(grad_t, w_rows, tokens_all):
     n, columns, tokens = grad_t.shape
     planes, _, width = tokens_all.shape
     rows, half = width // planes, n * columns // planes
-    copies = 2 * (n - 1) + 2 * (planes - 1) + PLANE_COPIES
+    copies = 2 * (n - 1) + planes - 1 + PLANE_COPIES
     bf, f32 = jnp.bfloat16, jnp.float32
     return pl.pallas_call(
         functools.partial(return_kernel, n, planes),
@@ -441,7 +498,9 @@
             pltpu.VMEM((planes, rows, half), bf),
             pltpu.SemaphoreType.DMA((copies,)),
             pltpu.SemaphoreType.DMA((copies,)),
-            pltpu.SemaphoreType.DMA((3,)),
+            pltpu.SemaphoreType.DMA((2 * n,)),
+            pltpu.SemaphoreType.DMA((planes,)),
+            pltpu.SemaphoreType.DMA((2,)),
         ],
         compiler_params=pltpu.CompilerParams(
             collective_id=2, has_side_effects=True, vmem_limit_bytes=36 << 20
@@ -450,19 +509,13 @@
 
 
 def body(layer_input, projected, grad_output, w_qkv, lengths, block_perm):
-    tokens_dev = layer_input.shape[1]
     width = layer_input.shape[2]
     ctx_count = lax.axis_size("ctx")
     data_count = lax.axis_size("dp")
     columns = 3 * DH
-    packed = jnp.concatenate(
-        [
-            projected[0].reshape(tokens_dev, ctx_count, columns),
-            grad_output[0].reshape(tokens_dev, ctx_count, DH),
-        ],
-        axis=2,
-    ).transpose(1, 0, 2)
-    blocks, tokens_all, w_rows = gather(packed, layer_input[0], w_qkv, data_count)
+    blocks, tokens_all, w_rows = gather(
+        projected[0], grad_output[0], layer_input[0], w_qkv, ctx_count, data_count
+    )
     grad_t = attention(blocks, lengths, block_perm)
     grad_input, parts = send_back(grad_t, w_rows, tokens_all)
     grad_weight = jnp.sum(parts.astype(jnp.float32), axis=0).transpose(1, 0, 2)

time: 175 us -> 172 us (0.983)
  Pallas kernels: 169 us -> 165 us
    pallas_call x1, Pallas kernels: 80.8 us -> 76.7 us  [send_back(): pl.pallas_call(functools.partial(return_kernel, n, planes), out_shape=(ja...]
    unnamed x11 -> x13, local copies, waits for them, and re-layouts: 3.4 us -> 5.75 us
where the time goes in v5:
time: 172 us
  Pallas kernels  165 us (96%)
  local copies, waits for them, and re-layouts  6.48 us (4%)
    pallas_call x1, Pallas kernels, send_back(): pl.pallas_call(functools.partial(return_kernel, n, planes), out_shape=(ja...  76.7 us
    pallas_call x1, Pallas kernels, gather(): pl.pallas_call(functools.partial(gather_kernel, n), out_shape=(jax.ShapeD...  74.2 us
    pallas_call x1, Pallas kernels, attention(): pl.pallas_call(functools.partial(attention_kernel, tile), out_shape=jax.S...  13.9 us
    unnamed x13, local copies, waits for them, and re-layouts  5.75 us

profile of v5, /device:TPU:1, one launch (start us, length us, event | category | flops | bytes accessed | tf_op | source)
XLA Modules:
  0.0 171.9 jit_solution(13046446837013221680)
XLA Ops:
  0.6 0.0 copy-start
  0.6 1.1 copy-done
  1.8 0.0 copy-start.1
  1.8 0.9 copy-done.1
  2.7 0.0 copy-start.2
  2.7 0.9 copy-done.2
  3.7 0.0 copy-start.3
  3.7 0.7 copy-done.3
  4.4 74.2 %shard_map.77 = (bf16[16,128,256]{2,1,0:T(8,128)(2,1)S(1)}, bf16[32,128,1024]{2,1,0:T(8,128)(2,1)S(1)}, bf16[16,32,192]{2,1,0:T(8,128)(2,1)S(1)}) custom-call(bf16[128,3072]{1,0:T(8,128)(2,1)S(1)} %bitcast.5, bf16[128,1024]{1,0:T(8,128)(2,1)S(1)} %bitcast.7, bf16[128,1024]{1,0:T(8,128)(2,1)S(1)} %bitcast.8, bf16[32,192]{1,0:T(8,128)(2,1)S(1)} %copy-done.3), custom_call_target="tpu_custom_call" | custom-call | tf_op jit(solution)/shard_map/pallas_call | solution.py:330
  78.6 0.0 copy-start.4
  78.6 0.6 copy-done.4
  79.2 0.0 copy-start.5
  79.2 0.7 copy-done.5
  79.9 13.9 %shard_map.78.grad_ref = bf16[16,192,128]{2,1,0:T(8,128)(2,1)S(1)} custom-call(s32[1,8]{1,0:T(1,128)S(1)} %copy-done.4, s32[1,16]{1,0:T(1,128)S(1)} %copy-done.5, bf16[16,128,256]{2,1,0:T(8,128)(2,1)S(1)} %get-tuple-element.7.x_ref), custom_call_target="tpu_custom_call" | custom-call | tf_op jit(solution)/shard_map/pallas_call | solution.py:120
  93.8 76.7 %shard_map.79 = (bf16[128,1024]{1,0:T(8,128)(2,1)S(1)}, bf16[16,2,32,96]{3,2,1,0:T(8,128)(2,1)S(1)}) custom-call(bf16[16,192,128]{2,1,0:T(8,128)(2,1)S(1)} %shard_map.78.grad_ref, bf16[16,32,192]{2,1,0:T(8,128)(2,1)S(1)} %get-tuple-element.8.w_rows_ref, bf16[32,128,1024]{2,1,0:T(8,128)(2,1)S(1)} %get-tuple-element.9.tokens_ref), custom_call_target="tpu_custom_call" | custom-call | tf_op jit(solution)/shard_map/pallas_call | solution.py:483
  170.4 0.1 convert_reduce_fusion
  170.5 0.7 reshape.7
  171.2 0.7 copy.10
  (1 shorter events, 0.0 us)
Async XLA Ops:
  0.6 1.1 copy-start
  1.8 0.9 copy-start.1
  2.7 0.9 copy-start.2
  3.7 0.7 copy-start.3
  78.6 0.7 copy-start.4
  79.2 0.7 copy-start.5

commit v6 on v5

--- a/solution.py
+++ b/solution.py
@@ -12,6 +12,7 @@
 LAG = 5
 MESH = pl.DeviceIdType.MESH
 VMEM = pl.BlockSpec(memory_space=pltpu.VMEM)
+HBM = pl.BlockSpec(memory_space=pltpu.HBM)
 
 
 def sigmoid(value):
@@ -284,7 +285,8 @@
 
 
 def gather_kernel(
-    n, pre_ref, grad_ref, tokens_ref, w_ref, recv_ref, tokens_all_ref, w_rows_ref, packed_ref, send_sem, recv_sem, local_sem
+    n, pre_hbm, grad_hbm, tokens_ref, w_ref, recv_ref, tokens_all_ref, w_rows_ref,
+    packed_ref, pre_ref, grad_ref, send_sem, recv_sem, local_sem,
 ):
     me = lax.axis_index("ctx")
     dp = lax.axis_index("dp")
@@ -297,7 +299,15 @@
     peers += [{"dp": (lax.rem(y + step, 4) * 4 + x) * 2 + core} for step in (1, 3)]
     barrier, count = greet(peers)
     links = Links(send_sem, recv_sem)
+    loads = [
+        pltpu.make_async_copy(pre_hbm, pre_ref, local_sem.at[3]),
+        pltpu.make_async_copy(grad_hbm, grad_ref, local_sem.at[4]),
+    ]
+    for copy in loads:
+        copy.start()
     columns = 3 * DH
+    for copy in loads:
+        copy.wait()
     for head in range(n):
         packed_ref[head, :, :columns] = pre_ref[:, head * columns : (head + 1) * columns]
         packed_ref[head, :, columns:] = grad_ref[:, head * DH : (head + 1) * DH]
@@ -334,28 +344,56 @@
             jax.ShapeDtypeStruct((planes,) + tokens.shape, tokens.dtype),
             jax.ShapeDtypeStruct((n,) + w.shape, w.dtype),
         ),
-        in_specs=[VMEM, VMEM, VMEM, VMEM],
+        in_specs=[HBM, HBM, HBM, HBM],
         out_specs=(VMEM, VMEM, VMEM),
         scratch_shapes=[
             pltpu.VMEM(packed, pre.dtype),
+            pltpu.VMEM(pre.shape, pre.dtype),
+            pltpu.VMEM(grads.shape, grads.dtype),
             pltpu.SemaphoreType.DMA((copies,)),
             pltpu.SemaphoreType.DMA((copies,)),
-            pltpu.SemaphoreType.DMA((3,)),
+            pltpu.SemaphoreType.DMA((5,)),
         ],
         compiler_params=pltpu.CompilerParams(
             collective_id=1, has_side_effects=True, vmem_limit_bytes=24 << 20
         ),
-    )(pre, grads, tokens, w)
+    )(*(pltpu.with_memory_space_constraint(array, pltpu.HBM) for array in (pre, grads, tokens, w)))
+
+
+def push(pending, src, dst, send_sem, recv_sem, device, here):
+    def remote():
+        return pltpu.make_async_remote_copy(
+            src_ref=src,
+            dst_ref=dst,
+            send_sem=send_sem,
+            recv_sem=recv_sem,
+            device_id=device,
+            device_id_type=MESH,
+        )
+
+    @pl.when(jnp.logical_not(here))
+    def _():
+        remote().start()
+
+    @pl.when(here)
+    def _():
+        pltpu.make_async_copy(src, dst, recv_sem).start()
+
+    pending.append((here, remote))
+
+
+def landed(ref, sem):
+    pltpu.make_async_copy(ref, ref, sem).wait()
 
 
 def return_kernel(
     n, planes, grad_ref, w_rows_ref, tokens_ref, input_ref, weight_ref,
-    back, cols, w_all, input_sum, weight_sum, parts, rows_in, send_sem, recv_sem, forward_send, forward_recv, local_sem,
+    back, cols, w_all, input_sum, weight_sum, parts, rows_in, heads_in, send_sem, recv_sem,
+    forward_send, forward_recv, local_sem,
 ):
     me = lax.axis_index("ctx")
     dp = lax.axis_index("dp")
     half = cols.shape[1]
-    pair = planes // n
     barrier, count = greet(ring_peers(me, n) + plane_peers(dp, planes))
     own_block = pltpu.make_async_copy(grad_ref.at[me], back.at[me], local_sem.at[0])
     own_block.start()
@@ -378,27 +416,10 @@
     def forward(head, place, source):
         for side in range(2):
             owner = head * 2 + side
-            chunk = source.at[head, pl.ds(side * half, half)]
-
-            def to_owner(chunk=chunk, owner=owner, side=side):
-                return pltpu.make_async_remote_copy(
-                    src_ref=chunk,
-                    dst_ref=cols.at[dp],
-                    send_sem=forward_send.at[2 * place + side],
-                    recv_sem=forward_recv.at[dp],
-                    device_id={"dp": owner},
-                    device_id_type=MESH,
-                )
-
-            @pl.when(owner != dp)
-            def _():
-                to_owner().start()
-
-            @pl.when(owner == dp)
-            def _():
-                pltpu.make_async_copy(chunk, cols.at[dp], forward_recv.at[dp]).start()
-
-            sent.append((owner, to_owner))
+            push(
+                pending, source.at[head, pl.ds(side * half, half)], cols.at[dp],
+                forward_send.at[2 * place + side], forward_recv.at[dp], {"dp": owner}, owner == dp,
+            )
 
     def add_head(head, carry):
         block = w_all[:, pl.ds(head, 1)].reshape(input_sum.shape[0], w_all.shape[3])
@@ -416,12 +437,12 @@
             chip = n - 1 if place == n - 1 else lax.rem(own_place - place + 2 * n - 2, n - 1)
             sources += [2 * chip, 2 * chip + 1]
         for source in sources:
-            pltpu.make_async_copy(cols.at[source], cols.at[source], forward_recv.at[source]).wait()
+            landed(cols.at[source], forward_recv.at[source])
         left = jnp.concatenate([cols[source] for source in sources], axis=1)
         right = jnp.concatenate([tokens_ref[source] for source in sources], axis=0)
         weight_sum[...] += jnp.dot(left, right, preferred_element_type=jnp.float32)
 
-    sent = []
+    pending = []
     forward(me, n - 1, grad_ref)
     plane = plane_gather(links, w_rows_ref, w_all)
     next(plane)
@@ -433,45 +454,50 @@
         if place >= added + LAG and added + 1 < n:
             add_sources(added)
             added += 2
-    for _ in plane:
-        pass
     own_block.wait()
-    own_rows.wait()
     while added < n:
         add_sources(added)
         added += 2
 
     mean = weight_sum[...] * (1.0 / planes)
     parts[...] = mean.T.astype(parts.dtype).reshape(parts.shape)
-    add_head(0, 0)
+    next(plane, None)
     own_part = pltpu.make_async_copy(parts.at[dp], rows_in.at[dp], local_sem.at[0])
     own_part.start()
     copies = all_to_all_start(links, "dp", dp, planes, parts, rows_in)
-    lax.fori_loop(1, 8, add_head, 0)
+    for _ in plane:
+        pass
+    own_rows.wait()
+    lax.fori_loop(0, 8, add_head, 0)
     own_part.wait()
     for copy in copies:
         copy.wait_recv()
 
     def head_rows(owner):
-        return rows_in.at[pl.ds(owner * pair, pair)]
-
-    own_head = pltpu.make_async_copy(head_rows(me), weight_ref.at[me], local_sem.at[1])
+        return rows_in.at[pl.ds(owner * 2, 2)]
+
+    own_head = pltpu.make_async_copy(head_rows(me), heads_in.at[me], local_sem.at[1])
     own_head.start()
     copies = []
     for step in far_first(n):
         owner = lax.rem(me + step, n)
-        copies.append(links.start(head_rows(owner), weight_ref.at[me], {"ctx": owner}))
+        copies.append(links.start(head_rows(owner), heads_in.at[me], {"ctx": owner}))
     lax.fori_loop(8, n, add_head, 0)
     input_ref[...] = input_sum[...].T.astype(input_ref.dtype)
     own_head.wait()
     for copy in copies:
         copy.wait_recv()
+    total = jnp.zeros(heads_in.shape[1:], jnp.float32)
+    for source in range(n):
+        total = total + heads_in[source].astype(jnp.float32)
+    weight_ref[:, :half] = total[0]
+    weight_ref[:, half:] = total[1]
     links.wait_sends()
-    for owner, to_owner in sent:
-
-        @pl.when(owner != dp)
+    for here, remote in pending:
+
+        @pl.when(jnp.logical_not(here))
         def _():
-            to_owner().wait_send()
+            remote().wait_send()
 
 
 def send_back(grad_t, w_rows, tokens_all):
@@ -484,7 +510,7 @@
         functools.partial(return_kernel, n, planes),
         out_shape=(
             jax.ShapeDtypeStruct((tokens, width), bf),
-            jax.ShapeDtypeStruct((n, planes // n, rows, half), bf),
+            jax.ShapeDtypeStruct((rows, columns), f32),
         ),
         in_specs=[VMEM, VMEM, VMEM],
         out_specs=(VMEM, VMEM),
@@ -496,6 +522,7 @@
             pltpu.VMEM((half, width), f32),
             pltpu.VMEM((planes, rows, half), bf),
             pltpu.VMEM((planes, rows, half), bf),
+            pltpu.VMEM((n, planes // n, rows, half), bf),
             pltpu.SemaphoreType.DMA((copies,)),
             pltpu.SemaphoreType.DMA((copies,)),
             pltpu.SemaphoreType.DMA((2 * n,)),
@@ -509,17 +536,13 @@
 
 
 def body(layer_input, projected, grad_output, w_qkv, lengths, block_perm):
-    width = layer_input.shape[2]
     ctx_count = lax.axis_size("ctx")
     data_count = lax.axis_size("dp")
-    columns = 3 * DH
     blocks, tokens_all, w_rows = gather(
         projected[0], grad_output[0], layer_input[0], w_qkv, ctx_count, data_count
     )
     grad_t = attention(blocks, lengths, block_perm)
-    grad_input, parts = send_back(grad_t, w_rows, tokens_all)
-    grad_weight = jnp.sum(parts.astype(jnp.float32), axis=0).transpose(1, 0, 2)
-    grad_weight = grad_weight.reshape(width // data_count, columns)
+    grad_input, grad_weight = send_back(grad_t, w_rows, tokens_all)
     return (grad_input[None], grad_weight)
 
 

time: 172 us -> 169 us (0.983)
  local copies, waits for them, and re-layouts: 6.48 us -> 2.62 us
    unnamed x13 -> x6, local copies, waits for them, and re-layouts: 5.75 us -> 2.62 us
where the time goes in v6:
time: 169 us
  Pallas kernels  165 us (98%)
  local copies, waits for them, and re-layouts  2.62 us (2%)
    pallas_call x1, Pallas kernels, send_back(): pl.pallas_call(functools.partial(return_kernel, n, planes), out_shape=(ja...  77.3 us
    pallas_call x1, Pallas kernels, gather(): pl.pallas_call(functools.partial(gather_kernel, n), out_shape=(jax.ShapeD...  74.2 us
    pallas_call x1, Pallas kernels, attention(): pl.pallas_call(functools.partial(attention_kernel, tile), out_shape=jax.S...  13.9 us

profile of v6, /device:TPU:1, one launch (start us, length us, event | category | flops | bytes accessed | tf_op | source)
XLA Modules:
  0.0 168.7 jit_solution(12319992632200107851)
XLA Ops:
  0.6 74.2 %shard_map.77 = (bf16[16,128,256]{2,1,0:T(8,128)(2,1)S(1)}, bf16[32,128,1024]{2,1,0:T(8,128)(2,1)S(1)}, bf16[16,32,192]{2,1,0:T(8,128)(2,1)S(1)}) custom-call(bf16[128,3072]{1,0:T(8,128)(2,1)} %bitcast.5, bf16[128,1024]{1,0:T(8,128)(2,1)} %bitcast.6, bf16[128,1024]{1,0:T(8,128)(2,1)} %bitcast.7, bf16[32,192]{1,0:T(8,128)(2,1)} %w_ref.1), custom_call_target="tpu_custom_call" | custom-call | tf_op jit(solution)/shard_map/pallas_call | solution.py:340
  74.8 0.0 copy-start
  74.8 0.6 copy-done
  75.5 0.0 copy-start.1
  75.5 0.7 copy-done.1
  76.1 13.9 %shard_map.78.grad_ref = bf16[16,192,128]{2,1,0:T(8,128)(2,1)S(1)} custom-call(s32[1,8]{1,0:T(1,128)S(1)} %copy-done, s32[1,16]{1,0:T(1,128)S(1)} %copy-done.1, bf16[16,128,256]{2,1,0:T(8,128)(2,1)S(1)} %get-tuple-element.7.x_ref), custom_call_target="tpu_custom_call" | custom-call | tf_op jit(solution)/shard_map/pallas_call | solution.py:121
  90.1 77.3 %shard_map.79 = (bf16[128,1024]{1,0:T(8,128)(2,1)S(1)}, f32[32,192]{1,0:T(8,128)S(1)}) custom-call(bf16[16,192,128]{2,1,0:T(8,128)(2,1)S(1)} %shard_map.78.grad_ref, bf16[16,32,192]{2,1,0:T(8,128)(2,1)S(1)} %get-tuple-element.8.w_rows_ref, bf16[32,128,1024]{2,1,0:T(8,128)(2,1)S(1)} %get-tuple-element.9.tokens_ref), custom_call_target="tpu_custom_call" | custom-call | tf_op jit(solution)/shard_map/pallas_call | solution.py:509
  167.4 0.7 copy.10
  168.1 0.6 copy.11
Async XLA Ops:
  74.8 0.7 copy-start
  75.5 0.7 copy-start.1

commit v7 on v6

--- a/solution.py
+++ b/solution.py
@@ -19,7 +19,15 @@
     return 0.5 * jnp.tanh(0.5 * value) + 0.5
 
 
-def attention_kernel(tile, lengths_ref, perm_ref, x_ref, out_ref, q_s, k_s, v_s, g_s, kt_s, gq_s, gk_s, gv_s, start_s, scale_s):
+def attention_kernel(tile, lengths_hbm, perm_hbm, x_ref, out_ref, q_s, k_s, v_s, g_s, kt_s, gq_s, gk_s, gv_s, start_s, scale_s, lengths_ref, perm_ref, sem):
+    loads = [
+        pltpu.make_async_copy(lengths_hbm, lengths_ref, sem.at[0]),
+        pltpu.make_async_copy(perm_hbm, perm_ref, sem.at[1]),
+    ]
+    for copy in loads:
+        copy.start()
+    for copy in loads:
+        copy.wait()
     slots = x_ref.shape[0]
     whole = slots * BLK
     users = lengths_ref.shape[1]
@@ -38,7 +46,7 @@
     start_s[...] = first
     scale_s[...] = lax.rsqrt(length.astype(jnp.float32))
 
-    @pl.loop(0, slots, unroll=4)
+    @pl.loop(0, slots, unroll=8)
     def _(slot):
         row = pl.multiple_of(perm_ref[0, slot] * BLK, BLK)
         block = x_ref[slot]
@@ -98,7 +106,7 @@
         gk_s[pl.ds(key_row, tile), :] = gk
         gv_s[pl.ds(key_row, tile), :] = gv
 
-    @pl.loop(0, slots, unroll=4)
+    @pl.loop(0, slots, unroll=8)
     def _(slot):
         row = pl.multiple_of(perm_ref[0, slot] * BLK, BLK)
         pre = x_ref[slot][:, : 3 * DH].astype(jnp.float32)
@@ -116,12 +124,13 @@
     slots = packed.shape[0]
     whole = slots * BLK
     vmem = pl.BlockSpec(memory_space=pltpu.VMEM)
-    smem = pl.BlockSpec(memory_space=pltpu.SMEM)
+    hbm = pl.BlockSpec(memory_space=pltpu.HBM)
+    lengths, perm = (pltpu.with_memory_space_constraint(array, pltpu.HBM) for array in (lengths, perm))
     bf, f32 = jnp.bfloat16, jnp.float32
     return pl.pallas_call(
         functools.partial(attention_kernel, tile),
         out_shape=jax.ShapeDtypeStruct((slots, 3 * DH, BLK), bf),
-        in_specs=[smem, smem, vmem],
+        in_specs=[hbm, hbm, vmem],
         out_specs=vmem,
         scratch_shapes=[
             pltpu.VMEM((whole, DH), bf),
@@ -134,6 +143,9 @@
             pltpu.VMEM((whole, DH), f32),
             pltpu.VMEM((whole // tile, tile), jnp.int32),
             pltpu.VMEM((whole // tile, tile), f32),
+            pltpu.SMEM(lengths.shape, jnp.int32),
+            pltpu.SMEM(perm.shape, jnp.int32),
+            pltpu.SemaphoreType.DMA((2,)),
         ],
         compiler_params=pltpu.CompilerParams(vmem_limit_bytes=24 << 20),
     )(lengths, perm, packed)
@@ -445,7 +457,8 @@
     pending = []
     forward(me, n - 1, grad_ref)
     plane = plane_gather(links, w_rows_ref, w_all)
-    next(plane)
+    for _ in range(5):
+        next(plane, None)
     added = 0
     for place, (head, copy) in enumerate(arrivals):
         copy.wait_recv()

time: 169 us -> 167 us (0.988)
    pallas_call x1, Pallas kernels: 13.9 us -> 11.9 us  [attention(): pl.pallas_call(functools.partial(attention_kernel, tile), out_shape=jax.S...]
where the time goes in v7:
time: 167 us
  Pallas kernels  165 us (99%)
    pallas_call x1, Pallas kernels, send_back(): pl.pallas_call(functools.partial(return_kernel, n, planes), out_shape=(ja...  78.9 us
    pallas_call x1, Pallas kernels, gather(): pl.pallas_call(functools.partial(gather_kernel, n), out_shape=(jax.ShapeD...  74.2 us
    pallas_call x1, Pallas kernels, attention(): pl.pallas_call(functools.partial(attention_kernel, tile), out_shape=jax.S...  11.9 us

profile of v7, /device:TPU:1, one launch (start us, length us, event | category | flops | bytes accessed | tf_op | source)
XLA Modules:
  0.0 166.9 jit_solution(14736827786572865991)
XLA Ops:
  0.6 74.2 %shard_map.77 = (bf16[16,128,256]{2,1,0:T(8,128)(2,1)S(1)}, bf16[32,128,1024]{2,1,0:T(8,128)(2,1)S(1)}, bf16[16,32,192]{2,1,0:T(8,128)(2,1)S(1)}) custom-call(bf16[128,3072]{1,0:T(8,128)(2,1)} %bitcast.5, bf16[128,1024]{1,0:T(8,128)(2,1)} %bitcast.6, bf16[128,1024]{1,0:T(8,128)(2,1)} %bitcast.7, bf16[32,192]{1,0:T(8,128)(2,1)} %w_ref.1), custom_call_target="tpu_custom_call" | custom-call | tf_op jit(solution)/shard_map/pallas_call | solution.py:352
  74.8 11.9 %shard_map.78.grad_ref = bf16[16,192,128]{2,1,0:T(8,128)(2,1)S(1)} custom-call(s32[1,8]{1,0:T(1,128)} %lengths_hbm.1, s32[1,16]{1,0:T(1,128)} %perm_hbm.1, bf16[16,128,256]{2,1,0:T(8,128)(2,1)S(1)} %get-tuple-element.7.x_ref), custom_call_target="tpu_custom_call" | custom-call | tf_op jit(solution)/shard_map/pallas_call | solution.py:130
  86.8 78.9 %shard_map.79 = (bf16[128,1024]{1,0:T(8,128)(2,1)S(1)}, f32[32,192]{1,0:T(8,128)S(1)}) custom-call(bf16[16,192,128]{2,1,0:T(8,128)(2,1)S(1)} %shard_map.78.grad_ref, bf16[16,32,192]{2,1,0:T(8,128)(2,1)S(1)} %get-tuple-element.8.w_rows_ref, bf16[32,128,1024]{2,1,0:T(8,128)(2,1)S(1)} %get-tuple-element.9.tokens_ref), custom_call_target="tpu_custom_call" | custom-call | tf_op jit(solution)/shard_map/pallas_call | solution.py:522
  165.6 0.7 copy.10
  166.3 0.6 copy.11

commit v8 on v7

--- a/solution.py
+++ b/solution.py
@@ -9,7 +9,7 @@
 
 DH = 64
 BLK = 128
-LAG = 5
+LAG = 3
 MESH = pl.DeviceIdType.MESH
 VMEM = pl.BlockSpec(memory_space=pltpu.VMEM)
 HBM = pl.BlockSpec(memory_space=pltpu.HBM)

time: 167 us -> 170 us (1.018)
  Pallas kernels: 165 us -> 168 us
    pallas_call x1, Pallas kernels: 78.9 us -> 82.1 us  [send_back(): pl.pallas_call(functools.partial(return_kernel, n, planes), out_shape=(ja...]
where the time goes in v8:
time: 170 us
  Pallas kernels  168 us (99%)
    pallas_call x1, Pallas kernels, send_back(): pl.pallas_call(functools.partial(return_kernel, n, planes), out_shape=(ja...  82.1 us
    pallas_call x1, Pallas kernels, gather(): pl.pallas_call(functools.partial(gather_kernel, n), out_shape=(jax.ShapeD...  74.2 us
    pallas_call x1, Pallas kernels, attention(): pl.pallas_call(functools.partial(attention_kernel, tile), out_shape=jax.S...  11.9 us

profile of v8, /device:TPU:1, one launch (start us, length us, event | category | flops | bytes accessed | tf_op | source)
XLA Modules:
  0.0 170.2 jit_solution(16462144404014897786)
XLA Ops:
  0.6 74.2 %shard_map.77 = (bf16[16,128,256]{2,1,0:T(8,128)(2,1)S(1)}, bf16[32,128,1024]{2,1,0:T(8,128)(2,1)S(1)}, bf16[16,32,192]{2,1,0:T(8,128)(2,1)S(1)}) custom-call(bf16[128,3072]{1,0:T(8,128)(2,1)} %bitcast.5, bf16[128,1024]{1,0:T(8,128)(2,1)} %bitcast.6, bf16[128,1024]{1,0:T(8,128)(2,1)} %bitcast.7, bf16[32,192]{1,0:T(8,128)(2,1)} %w_ref.1), custom_call_target="tpu_custom_call" | custom-call | tf_op jit(solution)/shard_map/pallas_call | solution.py:352
  74.8 11.9 %shard_map.78.grad_ref = bf16[16,192,128]{2,1,0:T(8,128)(2,1)S(1)} custom-call(s32[1,8]{1,0:T(1,128)} %lengths_hbm.1, s32[1,16]{1,0:T(1,128)} %perm_hbm.1, bf16[16,128,256]{2,1,0:T(8,128)(2,1)S(1)} %get-tuple-element.7.x_ref), custom_call_target="tpu_custom_call" | custom-call | tf_op jit(solution)/shard_map/pallas_call | solution.py:130
  86.8 82.1 %shard_map.79 = (bf16[128,1024]{1,0:T(8,128)(2,1)S(1)}, f32[32,192]{1,0:T(8,128)S(1)}) custom-call(bf16[16,192,128]{2,1,0:T(8,128)(2,1)S(1)} %shard_map.78.grad_ref, bf16[16,32,192]{2,1,0:T(8,128)(2,1)S(1)} %get-tuple-element.8.w_rows_ref, bf16[32,128,1024]{2,1,0:T(8,128)(2,1)S(1)} %get-tuple-element.9.tokens_ref), custom_call_target="tpu_custom_call" | custom-call | tf_op jit(solution)/shard_map/pallas_call | solution.py:522
  168.9 0.7 copy.10
  169.6 0.6 copy.11
